TPU v7x, 32 devices: a whole 2x2x4 slice. The times are simulated.
32 devices in a mesh: section: 2 (over core), block: 16 (over z, y, x).
Axes of the slice: x: 2, y: 2, z: 4, core: 2. Of those that a mesh axis runs over, the one named last changes fastest.
Arguments:
- state: float32 [2, 16, 5, 32, 1024], P('section', 'block'), may hold values from -1 to 3.5, as said below
- mean_flow: float32 [16, 5, 32, 1024], P('block'), may hold values from -0.5 to 1.5, as said below
- les_owner: int32 [16], replicated, may hold values from 0 to 15, each once
- ac_owner: int32 [16], replicated, may hold values from 0 to 15, each once
- les_nbr: int32 [16, 6], replicated, may hold values from -1 to 15, as said below
- ac_nbr: int32 [16, 6], replicated, may hold values from -1 to 15, as said below
- coupling: int32 [16], replicated, may hold values from 0 to 15, each once
Outputs:
- advanced: float32 [2, 16, 5, 32, 1024], P('section', 'block')
Inputs may be any that keep to these rules, and one draw needn't show every extreme that they name: `state`: section 0: density 1 to 1.5, momenta -0.4 to 0.4, pressure 0.4 (E - m.m / (2 r)) 0.7 to 1.3. Section 1: all entries -1 to 1. `mean_flow`: mean density 0.8 to 1.5, mean velocities -0.5 to 0.5, mean pressure 0.7 to 1.3. `les_nbr`: blocks sit on a 4 x 4 x 16/16 grid of equal blocks; an entry names the block beside it across that face, and that block names it back across the opposite face. `ac_nbr`: blocks sit on a 4 x 4 x 16/16 grid of equal blocks; an entry names the block beside it across that face, and that block names it back across the opposite face.
All inputs are finite; a program needn't handle non-finite values.
Results may differ from a plain program's by a relative error of at most 0.0003.
Values may be sent and summed in bfloat16 or wider, within the bound.
No kernel may reach another device: no remote copies, remote signals or barrier semaphores. Data moves between devices by JAX's collectives and lax.ppermute only.
A program may use at most 128 MiB of HBM per device.

v0:
```python
import jax
import jax.numpy as jnp
from jax import lax
from jax.sharding import PartitionSpec as P

STEPS = 2


GAMMA_LESS = 0.4
DT_LES = 0.2
DT_AC = 0.3
VISCOSITY = 0.05
FEEDBACK_GAIN = 0.5


def as_sent(array):
    return jax.tree.map(lambda a: a.astype(jnp.bfloat16) if a.dtype == jnp.float32 else a, array)


def partner_2(array, axis, stride):
    return lax.ppermute(array, axis, [(i, i ^ 1 << stride) for i in range(lax.axis_size(axis))])


def face_layers(volume):
    num_blocks, num_vars, cube_side, face_cells = volume.shape
    members = [
        volume[:, :, 0, :],
        volume[:, :, cube_side - 1, :],
        volume[:, :, :, 0:cube_side].reshape(num_blocks, num_vars, face_cells),
        volume[:, :, :, (cube_side - 1) * cube_side :].reshape(num_blocks, num_vars, face_cells),
        volume[:, :, :, 0::cube_side].reshape(num_blocks, num_vars, face_cells),
        volume[:, :, :, cube_side - 1 :: cube_side].reshape(num_blocks, num_vars, face_cells),
    ]
    return jnp.stack(members, axis=1)


def neighbours(volume, halo_cells):
    num_blocks, num_vars, cube_side, face_cells = volume.shape

    def face_grid(direction):
        return halo_cells[:, direction].reshape(num_blocks, num_vars, cube_side, cube_side)

    low_x = jnp.concatenate([halo_cells[:, 0][:, :, None, :], volume[:, :, :-1, :]], axis=2)
    high_x = jnp.concatenate([volume[:, :, 1:, :], halo_cells[:, 1][:, :, None, :]], axis=2)
    low_y = jnp.concatenate([face_grid(2), volume[:, :, :, :-cube_side]], axis=3)
    high_y = jnp.concatenate([volume[:, :, :, cube_side:], face_grid(3)], axis=3)
    z_index = lax.broadcasted_iota(jnp.int32, (1, 1, 1, face_cells), 3) % cube_side
    low_z = jnp.where(
        z_index == 0, jnp.repeat(face_grid(4), cube_side, axis=3), jnp.roll(volume, 1, axis=3)
    )
    high_z = jnp.where(
        z_index == cube_side - 1,
        jnp.repeat(face_grid(5), cube_side, axis=3),
        jnp.roll(volume, -1, axis=3),
    )
    return ((low_x, high_x), (low_y, high_y), (low_z, high_z))


def primitives(conserved):
    density = conserved[:, 0]
    momentum = conserved[:, 1:4]
    energy = conserved[:, 4]
    velocity = momentum / density[:, None]
    pressure = GAMMA_LESS * (energy - 0.5 * jnp.sum(momentum * velocity, axis=1))
    return (momentum, energy, velocity, pressure)


def flux_along(conserved, axis_k):
    momentum, energy, velocity, pressure = primitives(conserved)
    normal_speed = velocity[:, axis_k]
    members = [momentum[:, axis_k]]
    for component in range(3):
        entry_term = momentum[:, component] * normal_speed
        if component == axis_k:
            entry_term = entry_term + pressure
        members.append(entry_term)
    members.append((energy + pressure) * normal_speed)
    return (jnp.stack(members, axis=1), velocity)


def les_both(conserved, halo_cells):
    pairs = neighbours(conserved, halo_cells)
    momentum, energy, velocity, pressure = primitives(conserved)
    flux_sum = jnp.zeros_like(conserved)
    laplace = -6.0 * conserved
    gradient = []
    for axis_k in range(3):
        low_side, high_side = pairs[axis_k]
        flux_low, speed_low = flux_along(low_side, axis_k)
        flux_high, speed_high = flux_along(high_side, axis_k)
        flux_sum = flux_sum + 0.5 * (flux_high - flux_low)
        laplace = laplace + low_side + high_side
        gradient.append(0.5 * (speed_high - speed_low))
    vort_x = gradient[1][:, 2] - gradient[2][:, 1]
    vort_y = gradient[2][:, 0] - gradient[0][:, 2]
    vort_z = gradient[0][:, 1] - gradient[1][:, 0]
    lamb_vector = jnp.stack(
        [
            vort_y * velocity[:, 2] - vort_z * velocity[:, 1],
            vort_z * velocity[:, 0] - vort_x * velocity[:, 2],
            vort_x * velocity[:, 1] - vort_y * velocity[:, 0],
        ],
        axis=1,
    ).astype(jnp.bfloat16)
    updated = conserved + DT_LES * (VISCOSITY * laplace - flux_sum)
    return (updated, lamb_vector)


def resting(conserved, halo_cells):
    return (conserved, conserved[:, 1:4].astype(jnp.bfloat16))


def acoustic_advance(perturb, halo_cells, mean_state, source):
    pairs = neighbours(perturb, halo_cells)
    slopes = [0.5 * (high_side - low_side) for low_side, high_side in pairs]
    mean_density = mean_state[:, 0]
    mean_pressure = mean_state[:, 4]
    carried = (
        mean_state[:, 1][:, None] * slopes[0]
        + mean_state[:, 2][:, None] * slopes[1]
        + mean_state[:, 3][:, None] * slopes[2]
    )
    divergence = slopes[0][:, 1] + slopes[1][:, 2] + slopes[2][:, 3]
    members = [carried[:, 0] + mean_density * divergence]
    for axis_k in range(3):
        members.append(
            carried[:, 1 + axis_k] + slopes[axis_k][:, 4] / mean_density + source[:, axis_k]
        )
    members.append(carried[:, 4] + 1.4 * mean_pressure * divergence)
    return perturb - DT_AC * jnp.stack(members, axis=1)


def keep_les(advanced, halo_cells, mean_state, source):
    return advanced.at[:, 1:4].add(DT_LES * FEEDBACK_GAIN * source.astype(jnp.float32))


def acoustic_branch(advanced, halo_cells, mean_state, source):
    return acoustic_advance(advanced, halo_cells, mean_state, source.astype(jnp.float32))


def lookup_rows(lookup_table, positions):
    count = lookup_table.shape[0]
    matches = (positions[..., None] == lax.broadcasted_iota(jnp.int32, (count,), 0)).astype(
        jnp.int32
    )
    flat_table = lookup_table.reshape(count, -1)
    picked = jnp.sum(matches[..., None] * flat_table, axis=-2)
    return picked.reshape(positions.shape + lookup_table.shape[1:])


def invert(owner_list):
    count = owner_list.shape[0]
    slots = lax.broadcasted_iota(jnp.int32, (count, count), 0)
    blocks = lax.broadcasted_iota(jnp.int32, (count, count), 1)
    matches = (owner_list[None, :] == slots).astype(jnp.int32)
    return jnp.sum(matches * blocks, axis=1)


def on_device(state, mean_flow, les_owner, ac_owner, les_nbr, ac_nbr, coupling):
    section = lax.axis_index("section")
    device = lax.axis_index("block")
    devices = lax.axis_size("block")
    local_state = state[0]
    per_dev = local_state.shape[0]
    total_blocks = per_dev * devices
    les_side = section == 0
    owner_list = jnp.where(les_side, les_owner, ac_owner)
    partner_table = jnp.where(les_side, les_nbr, ac_nbr)
    inverse = invert(owner_list)
    partner = lookup_rows(partner_table, inverse)
    present = partner >= 0
    source_slot = lookup_rows(owner_list, jnp.maximum(partner, 0))
    opposite = jnp.bitwise_xor(lax.broadcasted_iota(jnp.int32, (1, 6), 1), 1)
    wanted = source_slot * 6 + opposite
    start_row = device * per_dev
    own_present = lax.dynamic_slice_in_dim(present, start_row, per_dev, 0)
    coupled = lookup_rows(les_owner, lookup_rows(coupling, invert(ac_owner)))
    feed_slot = lookup_rows(ac_owner, lookup_rows(invert(coupling), invert(les_owner)))
    pairing = jnp.where(les_side, feed_slot, coupled)
    current = local_state
    for step_index in range(STEPS):
        face_cells = face_layers(current)
        pieces = lax.all_to_all(
            as_sent(face_cells), "block", split_axis=3, concat_axis=0, tiled=True
        ).astype(face_cells.dtype)
        flattened = pieces.reshape((total_blocks * 6,) + pieces.shape[2:])
        chosen = jnp.take(flattened, wanted.reshape(-1), axis=0).reshape(
            (total_blocks, 6) + pieces.shape[2:]
        )
        arrived = lax.all_to_all(
            as_sent(chosen), "block", split_axis=0, concat_axis=3, tiled=True
        ).astype(chosen.dtype)
        halo_cells = jnp.where(own_present[:, :, None, None], arrived, face_cells)
        advanced, outgoing = lax.cond(les_side, les_both, resting, current, halo_cells)
        spread = lax.all_to_all(
            outgoing.reshape(per_dev, 3, -1), "block", split_axis=2, concat_axis=0, tiled=True
        )
        crossed = partner_2(spread, "section", 0)
        ordered = jnp.take(crossed, pairing, axis=0)
        source = lax.all_to_all(ordered, "block", split_axis=0, concat_axis=2, tiled=True).reshape(
            outgoing.shape
        )
        current = lax.cond(
            les_side, keep_les, acoustic_branch, advanced, halo_cells, mean_flow, source
        )
    return current[None]


def solution(mesh):
    return jax.shard_map(
        on_device,
        mesh=mesh,
        in_specs=(
            P("section", "block", None, None, None),
            P("block", None, None, None),
            P(),
            P(),
            P(),
            P(),
            P(),
        ),
        out_specs=P("section", "block", None, None, None),
        check_vma=False,
    )
```

profile of v0, /device:TPU:1, one launch (start us, length us, event | category | flops | bytes accessed | tf_op | source)
XLA Modules:
  0.0 734.2 jit_solution(10468378756829088406)
XLA Ops:
  9.1 2.4 copy.167
  11.5 3.8 reshape.3570
  15.3 7.4 %all-to-all-start = ((bf16[16,2,960]{2,1,0:T(2,128)(2,1)}), bf16[16,2,960]{2,1,0:T(2,128)(2,1)S(1)}, u32[]{:S(2)}, u32[]{:S(2)}) async-start(bf16[16,2,960]{2,1,0:T(2,128)(2,1)} %reshape.3570), calls=%async_computation | async-start | bytes 131072 | tf_op jit(solution)/shard_map/all_to_all | solution.py:183
  23.7 5.4 all-to-all-done
  29.1 3.3 reshape.3571
  32.3 3.4 copy.168
  38.1 3.5 all-to-all-start.1
  42.7 5.3 all-to-all-done.1
  49.3 8.5 %conditional.6 = (f32[1,5,32,1024]{3,2,1,0:T(8,128)S(1)}, bf16[1,3,32,1024]{3,2,1,0:T(8,128)(2,1)S(1)}) conditional(s32[]{:T(128)} %convert_element_type.153, (f32[1,5,32,1024]{3,0,2,1:T(1,128)S(1)}) %tuple.68, (f32[1,5,32,1024]{3,0,2,1:T(1,128)S(1)}, f32[1,6,5,1024]{3,0,2,1:T(1,128)}) %tuple.51), branch_computations={%region_3.5_spmd, %region_4.12_spmd} | conditional | flops 11122684 | bytes 68939792
  59.7 25.5 %copy.177 = bf16[1,3,32768]{1,0,2:T(2,128)(2,1)} copy(bf16[1,3,32768]{2,1,0:T(4,128)(2,1)S(1)} %reshape.3469) | data formatting | bytes 393216 | tf_op jit(solution)/shard_map/reshape | solution.py:196
  85.8 179.2 %reduce.75 = bf16[32768,3]{1,0:T(8,128)(2,1)} reduce(bf16[32768,1,3]{2,1,0:T(2,128)(2,1)} %bitcast.274, bf16[]{:T(256)} %broadcast.1274), dimensions={1}, to_apply=%bitcast.259.reduce_sub_computation | reduce | bytes 393218
  265.0 13.2 %reshape.3574 = bf16[16,2,3072]{2,1,0:T(2,128)(2,1)} reshape(bf16[32768,3]{1,0:T(8,128)(2,1)} %reduce.75) | data formatting | bytes 393216
  278.1 3.5 all-to-all-start.2
  282.3 6.2 all-to-all-done.2
  288.5 18.4 %reshape.3575 = bf16[32768,1,3]{2,1,0:T(2,128)(2,1)} reshape(bf16[16,2,3072]{2,1,0:T(2,128)(2,1)S(1)} %all-to-all-done.2) | data formatting | bytes 393216
  306.9 30.6 %copy.178 = bf16[1,3,32768]{2,1,0:T(4,128)(2,1)S(1)} copy(bf16[1,3,32768]{1,0,2:T(2,128)(2,1)} %bitcast.276) | data formatting | bytes 393216 | tf_op jit(solution)/shard_map/all_to_all | solution.py:195
  337.5 16.2 %collective-permute-start = (bf16[16,3,2048]{2,1,0:T(4,128)(2,1)S(1)}, bf16[16,3,2048]{2,1,0:T(4,128)(2,1)S(1)}, u32[]{:S(2)}, u32[]{:S(2)}) collective-permute-start(bf16[16,3,2048]{2,1,0:T(4,128)(2,1)S(1)} %bitcast.290), channel_id=1, source_target_pairs={{0,16},{16,0},{1,17},{17,1},{2,18},{18,2},{3,19},{19,3},{4,20},{20... | collective-permute-start | bytes 589832 | tf_op jit(solution)/shard_map/ppermute | solution.py:21
  355.9 11.1 %all_to_all.102 = bf16[16,3,2048]{2,1,0:T(4,128)(2,1)S(1)} all-to-all(bf16[16,3,2048]{2,1,0:T(4,128)(2,1)S(1)} %broadcast_select_fusion.1), channel_id=1, replica_groups=mesh['section'=2,'block'=16] {'block'}, dimensions={0} | all-to-all | bytes 393216 | tf_op jit(solution)/shard_map/all_to_all | solution.py:200
  367.2 20.2 %conditional.7 = (f32[1,5,32,1024]{3,2,1,0:T(8,128)S(1)}) conditional(s32[]{:T(128)} %convert_element_type.153, (f32[1,5,32,1024]{3,2,1,0:T(8,128)S(1)}, f32[1,6,5,1024]{3,0,2,1:T(1,128)}, f32[1,5,32,1024]{3,2,1,0:T(8,128)}, bf16[1,3,32,1024]{3,2,1,0:T(8,128)(2,1)S(1)}) %tuple.52, (f32[1,5,32,1024]{3,2,1,0:T(8,128)S(1)}, ...), branch_computations={%region_18.21_spmd, %region_19.22_spmd} | conditional | flops 4726783 | bytes 37875916 | solution.py:203
  368.7 2.2 slice_reduce_fusion.7
  393.1 10.7 %all_to_all.103 = bf16[16,2,960]{2,1,0:T(2,128)(2,1)S(1)} all-to-all(bf16[16,2,960]{2,1,0:T(2,128)(2,1)S(1)} %reshape.3576), channel_id=1, replica_groups=mesh['section'=2,'block'=16] {'block'}, dimensions={0} | all-to-all | bytes 122880 | tf_op jit(solution)/shard_map/all_to_all | solution.py:183
  403.9 2.3 reshape.3577
  409.6 9.2 %all_to_all.104 = bf16[16,2,960]{2,1,0:T(2,128)(2,1)S(1)} all-to-all(bf16[16,2,960]{2,1,0:T(2,128)(2,1)S(1)} %reshape.3578), channel_id=1, replica_groups=mesh['section'=2,'block'=16] {'block'}, dimensions={0} | all-to-all | bytes 122880 | tf_op jit(solution)/shard_map/all_to_all | solution.py:190
  420.8 25.5 %copy.191 = bf16[1,3,32768]{1,0,2:T(2,128)(2,1)} copy(bf16[1,3,32768]{2,1,0:T(4,128)(2,1)S(1)} %reshape.3471) | data formatting | bytes 393216 | tf_op jit(solution)/shard_map/reshape | solution.py:196
  446.4 179.2 %reduce.76 = bf16[32768,3]{1,0:T(8,128)(2,1)} reduce(bf16[32768,1,3]{2,1,0:T(2,128)(2,1)} %bitcast.275, bf16[]{:T(256)} %broadcast.1274), dimensions={1}, to_apply=%bitcast.265.reduce_sub_computation | reduce | bytes 393218
  625.5 12.5 %reshape.3580 = bf16[16,2,3072]{2,1,0:T(2,128)(2,1)S(1)} reshape(bf16[32768,3]{1,0:T(8,128)(2,1)} %reduce.76) | data formatting | bytes 393216
  638.0 9.5 %all_to_all.105 = bf16[16,2,3072]{2,1,0:T(2,128)(2,1)S(1)} all-to-all(bf16[16,2,3072]{2,1,0:T(2,128)(2,1)S(1)} %reshape.3580), channel_id=1, replica_groups=mesh['section'=2,'block'=16] {'block'}, dimensions={0} | all-to-all | bytes 393216 | tf_op jit(solution)/shard_map/all_to_all | solution.py:195
  647.6 18.4 %reshape.3581 = bf16[32768,1,3]{2,1,0:T(2,128)(2,1)} reshape(bf16[16,2,3072]{2,1,0:T(2,128)(2,1)S(1)} %all_to_all.105) | data formatting | bytes 393216
  666.0 30.6 %copy.192 = bf16[1,3,32768]{2,1,0:T(4,128)(2,1)S(1)} copy(bf16[1,3,32768]{1,0,2:T(2,128)(2,1)} %bitcast.277) | data formatting | bytes 393216 | tf_op jit(solution)/shard_map/all_to_all | solution.py:195
  696.6 2.6 collective-permute-start.1
  701.4 11.4 %all_to_all.106 = bf16[16,3,2048]{2,1,0:T(4,128)(2,1)S(1)} all-to-all(bf16[16,3,2048]{2,1,0:T(4,128)(2,1)S(1)} %broadcast_select_fusion), channel_id=1, replica_groups=mesh['section'=2,'block'=16] {'block'}, dimensions={0} | all-to-all | bytes 393216 | tf_op jit(solution)/shard_map/all_to_all | solution.py:200
  713.0 21.0 %conditional.17 = (f32[1,1,5,32,1024]{4,3,2,1,0:T(8,128)}) conditional(s32[]{:T(128)} %convert_element_type.153, (f32[1,5,32,1024]{3,2,1,0:T(8,128)S(1)}, f32[1,6,5,1024]{3,0,2,1:T(1,128)}, f32[1,5,32,1024]{3,2,1,0:T(8,128)}, bf16[1,3,32,1024]{3,2,1,0:T(8,128)(2,1)S(1)}) %tuple.55, (f32[1,5,32,1024]{3,2,1,0:T(8,128)S(1)}, ...), branch_computations={%region_28.31_spmd, %region_29.32_spmd} | conditional | flops 4726783 | bytes 37875916 | solution.py:203
  (217 shorter events, 72.1 us)
Async XLA Ops:
  7.9 14.8 %copy-start.27 = (s32[16]{0:T(128)S(1)}, s32[16]{0:T(128)}, u32[]{:S(2)}) copy-start(s32[16]{0:T(128)} %param.25) | copy-start | bytes 196
  7.9 14.8 %copy-start.28 = (s32[16]{0:T(128)S(1)}, s32[16]{0:T(128)}, u32[]{:S(2)}) copy-start(s32[16]{0:T(128)} %param.26) | copy-start | bytes 196
  7.9 15.0 %copy-start.23 = (s32[16,6]{0,1:T(8,128)S(1)}, s32[16,6]{0,1:T(8,128)}, u32[]{:S(2)}) copy-start(s32[16,6]{0,1:T(8,128)} %param.27) | copy-start | bytes 1156
  8.0 15.0 %copy-start.24 = (s32[16,6]{0,1:T(8,128)S(1)}, s32[16,6]{0,1:T(8,128)}, u32[]{:S(2)}) copy-start(s32[16,6]{0,1:T(8,128)} %param.28) | copy-start | bytes 1156
  15.3 13.8 %all-to-all-start = ((bf16[16,2,960]{2,1,0:T(2,128)(2,1)}), bf16[16,2,960]{2,1,0:T(2,128)(2,1)S(1)}, u32[]{:S(2)}, u32[]{:S(2)}) async-start(bf16[16,2,960]{2,1,0:T(2,128)(2,1)} %reshape.3570), calls=%async_computation | async-start | bytes 131072 | tf_op jit(solution)/shard_map/all_to_all | solution.py:183
  23.7 13.4 %copy-start.25 = (pred[96]{0:T(512)(128)(4,1)}, pred[96]{0:T(512)(128)(4,1)S(1)}, u32[]{:S(2)}) copy-start(pred[96]{0:T(512)(128)(4,1)S(1)} %compare_and_fusion.1) | copy-start | bytes 292
  23.7 13.2 %copy-start.17 = (s32[1024]{0:T(1024)}, s32[1024]{0:T(1024)S(1)}, u32[]{:S(2)}) copy-start(s32[1024]{0:T(1024)S(1)} %pad_clamp_fusion.1) | copy-start | bytes 12292
  32.3 9.3 %copy-start.30 = (s32[16]{0:T(128)S(1)}, s32[16]{0:T(128)}, u32[]{:S(2)}) copy-start(s32[16]{0:T(128)} %param.29) | copy-start | bytes 196
  38.1 9.9 %all-to-all-start.1 = ((bf16[16,2,960]{2,1,0:T(2,128)(2,1)}), bf16[16,2,960]{2,1,0:T(2,128)(2,1)S(1)}, u32[]{:S(2)}, u32[]{:S(2)}) async-start(bf16[16,2,960]{2,1,0:T(2,128)(2,1)} %reshape.3572), calls=%async_computation.1 | async-start | bytes 131072 | tf_op jit(solution)/shard_map/all_to_all | solution.py:190
  42.0 7.3 copy-start.21
  265.0 16.7 %copy-start.29 = (s32[16]{0:T(128)S(1)}, s32[16]{0:T(128)}, u32[]{:S(2)}) copy-start(s32[16]{0:T(128)} %param.26) | copy-start | bytes 196
  265.0 16.8 %copy-start.32 = (s32[16]{0:T(128)S(1)}, s32[16]{0:T(128)}, u32[]{:S(2)}) copy-start(s32[16]{0:T(128)} %select_reduce_fusion.5) | copy-start | bytes 196
  265.0 17.0 %copy-start.31 = (s32[16]{0:T(128)S(1)}, s32[16]{0:T(128)}, u32[]{:S(2)}) copy-start(s32[16]{0:T(128)} %param.29) | copy-start | bytes 196
  278.1 10.4 %all-to-all-start.2 = ((bf16[16,2,3072]{2,1,0:T(2,128)(2,1)}), bf16[16,2,3072]{2,1,0:T(2,128)(2,1)S(1)}, u32[]{:S(2)}, u32[]{:S(2)}) async-start(bf16[16,2,3072]{2,1,0:T(2,128)(2,1)} %reshape.3574), calls=%async_computation.2 | async-start | bytes 393216 | tf_op jit(solution)/shard_map/all_to_all | solution.py:195
  337.5 17.3 %collective-permute-start = (bf16[16,3,2048]{2,1,0:T(4,128)(2,1)S(1)}, bf16[16,3,2048]{2,1,0:T(4,128)(2,1)S(1)}, u32[]{:S(2)}, u32[]{:S(2)}) collective-permute-start(bf16[16,3,2048]{2,1,0:T(4,128)(2,1)S(1)} %bitcast.290), channel_id=1, source_target_pairs={{0,16},{16,0},{1,17},{17,1},{2,18},{18,2},{3,19},{19,3},{4,20},{20... | collective-permute-start | bytes 589832 | tf_op jit(solution)/shard_map/ppermute | solution.py:21
  353.7 13.5 %copy-start.19 = (pred[16]{0:T(512)(128)(4,1)}, pred[16]{0:T(512)(128)(4,1)S(1)}, u32[]{:S(2)}) copy-start(pred[16]{0:T(512)(128)(4,1)S(1)} %get-tuple-element.162) | copy-start | bytes 52
  353.7 13.5 %copy-start.18 = (s32[1024]{0:T(1024)}, s32[1024]{0:T(1024)S(1)}, u32[]{:S(2)}) copy-start(s32[1024]{0:T(1024)S(1)} %pad_clamp_fusion) | copy-start | bytes 12292
  376.0 2.6 copy-start.14
  383.0 2.1 copy-start
  385.1 1.3 copy-start.3
  385.1 1.3 copy-start.8
  385.1 1.3 copy-start.10
  385.1 1.3 copy-start.11
  403.9 5.3 copy-start.26
  407.7 11.5 %copy-start.22 = (pred[6]{0:T(512)(128)(4,1)S(1)}, pred[6]{0:T(512)(128)(4,1)}, u32[]{:S(2)}) copy-start(pred[6]{0:T(512)(128)(4,1)} %copy-done.21) | copy-start | bytes 22
  666.0 35.3 %copy-start.20 = (pred[16]{0:T(512)(128)(4,1)S(1)}, pred[16]{0:T(512)(128)(4,1)}, u32[]{:S(2)}) copy-start(pred[16]{0:T(512)(128)(4,1)} %copy-done.19) | copy-start | bytes 52
  696.6 3.8 collective-permute-start.1
  721.8 2.6 copy-start.15
  728.8 2.1 copy-start.1
  730.9 1.3 copy-start.5
  730.9 1.3 copy-start.9
  730.9 1.3 copy-start.12
  (4 other events, 4.1 us)
where the time goes:
time: 742 us; the launch traced here: 734 us
  other arithmetic  374 us (50%)
  local copies, waits for them, and re-layouts  246 us (33%)
  blocking collectives  51.9 us (7%)
  starting transfers between devices  33.2 us (4%)
  waiting for transfers between devices  19.1 us (3%)
  loops' own time  9.39 us (1%)
    unnamed x2, other arithmetic  358 us
    unnamed x57, local copies, waits for them, and re-layouts  76.4 us
    all_to_all x2, local copies, waits for them, and re-layouts, on_device(): lax.all_to_all(outgoing.reshape(per_dev, 3, -1), 'block', split_axis=2, c...  61.2 us
    reshape x4, local copies, waits for them, and re-layouts, on_device(): outgoing.reshape(per_dev, 3, -1)  52.5 us
    all_to_all x2, blocking collectives, on_device(): lax.all_to_all(ordered, 'block', split_axis=0, concat_axis=2, tiled=True)  22.5 us
    ppermute x2, starting transfers between devices, partner_2(): lax.ppermute(array, axis, [(i, i ^ 1 << stride) for i in range(lax.axis_s...  18.8 us
  transfers between devices with their start and end apart: 5, of which 5 were waited for; matrix products, arithmetic and copies ran while one was open for 0% of the time, Pallas kernels for 0%

commit v1 on v0

v1 whole, which is shorter than its diff:
```python
import functools

import jax
import jax.numpy as jnp
from jax import lax
from jax.experimental import pallas as pl
from jax.experimental.pallas import tpu as pltpu
from jax.sharding import PartitionSpec as P


STEPS = 2

GAMMA_LESS = 0.4
DT_LES = 0.2
DT_AC = 0.3
VISCOSITY = 0.05
FEEDBACK_GAIN = 0.5

WIRE = jnp.int16
SCALE_IN = 32000.0
SCALE_MID = 8192.0
SCALE_OUT = 4096.0
OFFSETS = ((1.25, 0.0, 0.0, 0.0, 2.6), (0.0, 0.0, 0.0, 0.0, 0.0))
MEAN_OFFSETS = (1.0, 0.0, 0.0, 0.0, 1.0)
PAIRS = ((0, 1), (2, 3), (4, 4))

LANES = 128
FACES = 6
COLUMNS = FACES + 1


class Plan:
    def __init__(self, blocks, sections, num_vars, side):
        self.blocks = blocks
        self.devices = blocks * sections
        self.vars = num_vars
        self.side = side
        self.layers_z = blocks // 16
        self.ny = side * side // LANES
        self.nx = self.devices // self.ny
        self.xs = side // self.nx
        self.half = self.xs // sections
        self.core_rows = num_vars * self.xs
        self.y_base = self.core_rows
        self.mean_base = self.y_base + len(PAIRS) * self.xs
        self.x_base = self.mean_base + num_vars * self.half
        self.rows = -(-(self.x_base + 2 * num_vars) // 16) * 16
        assert sections == 2 and LANES == 4 * side and 2 * self.half * self.nx == side

    def piece(self, device):
        section, block = device // self.blocks, device % self.blocks
        low, mid, high = block % 2, block // 2 % 2, block // 4
        ring = section if low == 0 else 3 - section
        depth = high % 4
        return ring + 4 * (high // 4), depth if mid == 0 else 7 - depth

    def own_piece(self, section, block):
        low, mid, high = block % 2, block // 2 % 2, block // 4
        ring = jnp.where(low == 0, section, 3 - section)
        depth = high % 4
        return ring + 4 * (high // 4), jnp.where(mid == 0, depth, 7 - depth)

    def permutation(self, step_x, step_y):
        at = {self.piece(d): d for d in range(self.devices)}
        assert len(at) == self.devices
        pairs = []
        for device in range(self.devices):
            px, py = self.piece(device)
            pairs.append((device, at[((px + step_x) % self.nx, (py + step_y) % self.ny)]))
        return pairs


def to_wire(scaled):
    return lax.round(scaled, lax.RoundingMethod.TO_NEAREST_EVEN).astype(jnp.int32).astype(WIRE)


def from_wire(sent):
    return sent.astype(jnp.int32).astype(jnp.float32)


def roll_lanes(tile, shift):
    return pltpu.roll(tile, shift % LANES, 1)


def roll_rows(tile, shift):
    rows = tile.shape[0]
    shift = shift % rows
    if rows % 8 == 0:
        return pltpu.roll(tile, shift, 0)
    return jnp.concatenate([tile[rows - shift :], tile[: rows - shift]], axis=0)


def lane_index(rows):
    return lax.broadcasted_iota(jnp.int32, (rows, LANES), 1)


def pack_kernel(
    plan, state, mean, les_owner, ac_owner, les_nbr, ac_nbr, coupling,
    message, table, raw, filled, les_inv, ac_inv, pair_inv,
):
    section = lax.axis_index("section")
    px, py = plan.own_piece(section, lax.axis_index("block"))
    xs, side, half = plan.xs, plan.side, plan.half
    width = side * side
    for v in range(plan.vars):
        offset = jnp.where(section == 0, OFFSETS[0][v], OFFSETS[1][v])
        raw[v] = (state[v] - offset) * SCALE_IN
    lane = lane_index(xs)
    for device in range(plan.devices):
        tx, ty = plan.piece(device)
        x0, l0 = tx * xs, ty * LANES
        here = slice(l0, l0 + LANES)
        before = (l0 - LANES) % width
        after = (l0 + LANES) % width
        for v in range(plan.vars):
            filled[device, v * xs : (v + 1) * xs, :] = raw[v, x0 : x0 + xs, here]
            filled[device, plan.x_base + v, :] = raw[v, (x0 - 1) % side, here]
            filled[device, plan.x_base + plan.vars + v, :] = raw[v, (x0 + xs) % side, here]
            first, second = mean[v, x0 : x0 + half, here], mean[v, x0 + half : x0 + xs, here]
            piece = jnp.where(section == 0, first, second)
            base = plan.mean_base + v * half
            filled[device, base : base + half, :] = (piece - MEAN_OFFSETS[v]) * SCALE_IN
        for i, (a, b) in enumerate(PAIRS):
            low_a = raw[a, x0 : x0 + xs, before : before + LANES]
            low_b = raw[b, x0 : x0 + xs, before : before + LANES]
            high_a = raw[a, x0 : x0 + xs, after : after + LANES]
            high_b = raw[b, x0 : x0 + xs, after : after + LANES]
            low = jnp.where(lane < side, roll_lanes(low_a, side), roll_lanes(high_b, side))
            high = jnp.where(lane < 3 * side, roll_lanes(low_b, -side), roll_lanes(high_a, -side))
            base = plan.y_base + i * xs
            filled[device, base : base + xs, :] = jnp.where(lane < 2 * side, low, high)
        used = plan.x_base + 2 * plan.vars
        if used < plan.rows:
            filled[device, used:, :] = jnp.zeros((plan.rows - used, LANES), jnp.float32)
        message[device] = to_wire(filled[device])

    def invert(i, carry):
        les_inv[les_owner[i]] = i
        ac_inv[ac_owner[i]] = i
        pair_inv[coupling[i]] = i
        return carry

    lax.fori_loop(0, plan.blocks, invert, 0)
    at_edge = (px == 0, px == plan.nx - 1, py == 0, py == plan.ny - 1, True, True)

    def look_up(slot, carry):
        les_block = les_inv[slot]
        ac_block = ac_inv[slot]
        for kind, (block, nbr, owner) in enumerate(
            ((les_block, les_nbr, les_owner), (ac_block, ac_nbr, ac_owner))
        ):
            for face in range(FACES):
                other = nbr[block, face]
                source = jnp.where(other < 0, -1, owner[jnp.maximum(other, 0)])
                if face < 4:
                    source = jnp.where(at_edge[face], source, slot)
                table[(kind * COLUMNS + face) * plan.blocks + slot] = source
        table[FACES * plan.blocks + slot] = ac_owner[pair_inv[les_block]]
        table[(COLUMNS + FACES) * plan.blocks + slot] = les_owner[coupling[ac_block]]
        return carry

    lax.fori_loop(0, plan.blocks, look_up, 0)


def sides(plan, table, kind, slot, core, x_halo, y_halo):
    xs, side = plan.xs, plan.side
    lane = lane_index(xs)
    row = lax.broadcasted_iota(jnp.int32, (xs, LANES), 0)
    depth = lane % side
    found = [table[(kind * COLUMNS + face) * plan.blocks + slot] for face in range(FACES)]
    inside = [f >= 0 for f in found]
    found = [jnp.maximum(f, 0) for f in found]
    own = [core(kind, slot, v) for v in range(plan.vars)]
    shifted = [[] for _ in range(FACES)]
    for v, tile in enumerate(own):
        low = jnp.where(inside[0], x_halo(kind, found[0], v, 0), tile[0:1])
        high = jnp.where(inside[1], x_halo(kind, found[1], v, 1), tile[xs - 1 : xs])
        shifted[0].append(jnp.where(row == 0, low, roll_rows(tile, 1)))
        shifted[1].append(jnp.where(row == xs - 1, high, roll_rows(tile, -1)))
        low = jnp.where(inside[2], y_halo(kind, found[2], v, 0), tile)
        high = jnp.where(inside[3], y_halo(kind, found[3], v, 1), tile)
        shifted[2].append(jnp.where(lane < side, low, roll_lanes(tile, side)))
        shifted[3].append(jnp.where(lane >= LANES - side, high, roll_lanes(tile, -side)))
        low, high = tile, tile
        if plan.layers_z > 1:
            low = jnp.where(inside[4], roll_lanes(core(kind, found[4], v), 1 - side), tile)
            high = jnp.where(inside[5], roll_lanes(core(kind, found[5], v), side - 1), tile)
        shifted[4].append(jnp.where(depth == 0, low, roll_lanes(tile, 1)))
        shifted[5].append(jnp.where(depth == side - 1, high, roll_lanes(tile, -1)))
    return own, shifted


def primitives(conserved):
    density, energy = conserved[0], conserved[4]
    momentum = conserved[1:4]
    inverse = 1.0 / density
    velocity = [m * inverse for m in momentum]
    kinetic = momentum[0] * velocity[0] + momentum[1] * velocity[1] + momentum[2] * velocity[2]
    return momentum, energy, velocity, GAMMA_LESS * (energy - 0.5 * kinetic)


def flux_along(conserved, axis):
    momentum, energy, velocity, pressure = primitives(conserved)
    normal = velocity[axis]
    flux = [momentum[axis]]
    for component in range(3):
        entry = momentum[component] * normal
        flux.append(entry + pressure if component == axis else entry)
    flux.append((energy + pressure) * normal)
    return flux, velocity


def cross(a, b):
    return [
        a[1] * b[2] - a[2] * b[1],
        a[2] * b[0] - a[0] * b[2],
        a[0] * b[1] - a[1] * b[0],
    ]


def as_bf16(tile):
    return tile.astype(jnp.bfloat16).astype(jnp.float32)


def les_slot(plan, own, shifted):
    count = plan.vars
    total = [(1.0 - 6.0 * DT_LES * VISCOSITY) * own[v] for v in range(count)]
    gradient = []
    for axis in range(3):
        low, high = shifted[2 * axis], shifted[2 * axis + 1]
        flux_low, speed_low = flux_along(low, axis)
        flux_high, speed_high = flux_along(high, axis)
        for v in range(count):
            total[v] = total[v] + (
                DT_LES * VISCOSITY * (low[v] + high[v]) - 0.5 * DT_LES * (flux_high[v] - flux_low[v])
            )
        gradient.append([0.5 * (h - w) for h, w in zip(speed_high, speed_low)])
    velocity = [m * (1.0 / own[0]) for m in own[1:4]]
    vorticity = [
        gradient[1][2] - gradient[2][1],
        gradient[2][0] - gradient[0][2],
        gradient[0][1] - gradient[1][0],
    ]
    return total, [as_bf16(t) for t in cross(vorticity, velocity)]


def ac_slot(plan, own, shifted, mean, source):
    slope = [
        [0.5 * (h - w) for h, w in zip(shifted[2 * axis + 1], shifted[2 * axis])] for axis in range(3)
    ]
    carried = [
        mean[1] * slope[0][v] + mean[2] * slope[1][v] + mean[3] * slope[2][v]
        for v in range(plan.vars)
    ]
    divergence = slope[0][1] + slope[1][2] + slope[2][3]
    inverse = 1.0 / mean[0]
    change = [carried[0] + mean[0] * divergence]
    for axis in range(3):
        change.append(carried[1 + axis] + slope[axis][4] * inverse + source[axis])
    change.append(carried[4] + 1.4 * mean[4] * divergence)
    return [g - DT_AC * c for g, c in zip(own, change)]


def advance(plan, table, core, x_halo, y_halo, mean, lamb, store):
    xs = plan.xs

    def les_body(slot, carry):
        own, shifted = sides(plan, table, 0, slot, core, x_halo, y_halo)
        total, vector = les_slot(plan, own, shifted)
        partner = table[FACES * plan.blocks + slot]
        for j in range(3):
            back = as_bf16(core(1, partner, 1 + j))
            total[1 + j] = total[1 + j] + DT_LES * FEEDBACK_GAIN * back
            lamb[slot, j * xs : (j + 1) * xs, :] = vector[j]
        store(0, slot, total)
        return carry

    def ac_body(slot, carry):
        own, shifted = sides(plan, table, 1, slot, core, x_halo, y_halo)
        partner = table[(COLUMNS + FACES) * plan.blocks + slot]
        source = [lamb[partner, j * xs : (j + 1) * xs, :] for j in range(3)]
        store(1, slot, ac_slot(plan, own, shifted, mean(slot), source))
        return carry

    lax.fori_loop(0, plan.blocks, les_body, 0, unroll=2)
    lax.fori_loop(0, plan.blocks, ac_body, 0, unroll=2)


def tile_rows(plan, v):
    return slice(v * plan.xs, (v + 1) * plan.xs)


def first_kernel(
    plan, table, message,
    after, mean_out, x_up, x_down, y_up, y_down,
    arrived, lamb, x_up_raw, x_down_raw, y_up_raw, y_down_raw,
):
    xs, side, count, blocks, half = plan.xs, plan.side, plan.vars, plan.blocks, plan.half
    lane = lane_index(xs)

    def read(m, carry):
        arrived[m] = from_wire(message[m]) * (1.0 / SCALE_IN)
        return carry

    lax.fori_loop(0, plan.devices, read, 0, unroll=2)

    def read_mean(slot, carry):
        for v in range(count):
            base = plan.mean_base + v * half
            for part in range(plan.devices // blocks):
                rows = arrived[part * blocks + slot, base : base + half, :]
                start = v * xs + part * half
                mean_out[slot, start : start + half, :] = rows + MEAN_OFFSETS[v]
        return carry

    lax.fori_loop(0, blocks, read_mean, 0)

    def shift_back(tile, kind, v):
        return tile if OFFSETS[kind][v] == 0.0 else tile + OFFSETS[kind][v]

    def core(kind, slot, v):
        return shift_back(arrived[kind * blocks + slot, tile_rows(plan, v), :], kind, v)

    def x_halo(kind, slot, v, end):
        at = plan.x_base + end * count + v
        return shift_back(arrived[kind * blocks + slot, at : at + 1, :], kind, v)

    def y_halo(kind, slot, v, end):
        base = plan.y_base + (v // 2) * xs
        tile = arrived[kind * blocks + slot, base : base + xs, :]
        if v % 2 == 1:
            tile = roll_lanes(tile, 2 * side)
        return shift_back(tile, kind, v)

    def mean(slot):
        return [mean_out[slot, tile_rows(plan, v), :] for v in range(count)]

    def store(kind, slot, tiles):
        m = kind * blocks + slot
        quarter = m % 4
        rest = plan.devices * xs + (m // 4) * xs
        up = down = None
        for v, tile in enumerate(tiles):
            after[m, tile_rows(plan, v), :] = tile
            coded = (tile - OFFSETS[kind][v]) * SCALE_MID
            x_up_raw[pl.ds(m * count + v, 1), :] = coded[xs - 1 : xs]
            x_down_raw[pl.ds(m * count + v, 1), :] = coded[0:1]
            if v < 4:
                high = roll_lanes(coded, side * (v + 1))
                low = roll_lanes(coded, side * v)
                mine = lane >= side * v
                up = high if v == 0 else jnp.where(mine, high, up)
                down = low if v == 0 else jnp.where(mine, low, down)
            else:
                high = pltpu.roll(coded, (side * (quarter + 1)) % LANES, 1)
                low = pltpu.roll(coded, side * quarter, 1)
                mine = lane >= side * quarter
                where = pl.ds(pl.multiple_of(rest, xs), xs)
                y_up_raw[where, :] = jnp.where(mine, high, y_up_raw[where, :])
                y_down_raw[where, :] = jnp.where(mine, low, y_down_raw[where, :])
        where = pl.ds(pl.multiple_of(m * xs, xs), xs)
        y_up_raw[where, :] = up
        y_down_raw[where, :] = down

    advance(plan, table, core, x_halo, y_halo, mean, lamb, store)
    for raw, out in (
        (x_up_raw, x_up), (x_down_raw, x_down), (y_up_raw, y_up), (y_down_raw, y_down),
    ):
        out[...] = to_wire(raw[...])


def last_kernel(
    plan, table, before, mean_in, x_low, x_high, y_low, y_high,
    message, lamb, x_low_raw, x_high_raw, y_low_raw, y_high_raw, coded,
):
    xs, side, count, blocks = plan.xs, plan.side, plan.vars, plan.blocks
    for raw, sent in (
        (x_low_raw, x_low), (x_high_raw, x_high), (y_low_raw, y_low), (y_high_raw, y_high),
    ):
        raw[...] = from_wire(sent[...]) * (1.0 / SCALE_MID)

    def shift_back(tile, kind, v):
        return tile if OFFSETS[kind][v] == 0.0 else tile + OFFSETS[kind][v]

    def core(kind, slot, v):
        return before[kind * blocks + slot, tile_rows(plan, v), :]

    def x_halo(kind, slot, v, end):
        raw = x_high_raw if end else x_low_raw
        return shift_back(raw[pl.ds((kind * blocks + slot) * count + v, 1), :], kind, v)

    def y_halo(kind, slot, v, end):
        raw = y_high_raw if end else y_low_raw
        m = kind * blocks + slot
        target = 3 * side if end else 0
        if v < 4:
            tile = raw[pl.ds(pl.multiple_of(m * xs, xs), xs), :]
            tile = roll_lanes(tile, target - side * v)
        else:
            rest = plan.devices * xs + (m // 4) * xs
            tile = raw[pl.ds(pl.multiple_of(rest, xs), xs), :]
            tile = pltpu.roll(tile, (target + LANES - side * (m % 4)) % LANES, 1)
        return shift_back(tile, kind, v)

    def mean(slot):
        return [mean_in[slot, tile_rows(plan, v), :] for v in range(count)]

    def store(kind, slot, tiles):
        for v, tile in enumerate(tiles):
            coded[kind * blocks + slot, tile_rows(plan, v), :] = (tile - OFFSETS[kind][v]) * SCALE_OUT

    advance(plan, table, core, x_halo, y_halo, mean, lamb, store)

    def write(m, carry):
        message[m] = to_wire(coded[m])
        return carry

    lax.fori_loop(0, plan.devices, write, 0, unroll=2)


def unpack_kernel(plan, message, out):
    section = lax.axis_index("section")
    xs = plan.xs
    for device in range(plan.devices):
        tx, ty = plan.piece(device)
        values = from_wire(message[device]) * (1.0 / SCALE_OUT)
        for v in range(plan.vars):
            offset = jnp.where(section == 0, OFFSETS[0][v], OFFSETS[1][v])
            out[v, tx * xs : (tx + 1) * xs, ty * LANES : (ty + 1) * LANES] = (
                values[v * xs : (v + 1) * xs] + offset
            )


def vmem(count):
    return [pl.BlockSpec(memory_space=pltpu.VMEM)] * count


def smem(count):
    return [pl.BlockSpec(memory_space=pltpu.SMEM)] * count


def on_device(plan, state, mean_flow, les_owner, ac_owner, les_nbr, ac_nbr, coupling):
    axes = ("section", "block")
    devices, blocks, count, xs = plan.devices, plan.blocks, plan.vars, plan.xs
    f32 = jnp.float32

    def array(dtype, *shape):
        return jax.ShapeDtypeStruct(shape, dtype)

    message, table = pl.pallas_call(
        functools.partial(pack_kernel, plan),
        out_shape=(
            array(WIRE, devices, plan.rows, LANES),
            array(jnp.int32, 2 * COLUMNS * blocks),
        ),
        in_specs=vmem(2) + smem(5),
        out_specs=tuple(vmem(1) + smem(1)),
        scratch_shapes=[
            pltpu.VMEM((count, plan.side, plan.side * plan.side), f32),
            pltpu.VMEM((devices, plan.rows, LANES), f32),
        ]
        + [pltpu.SMEM((blocks,), jnp.int32)] * 3,
        name="pack",
    )(state[0, 0], mean_flow[0], les_owner, ac_owner, les_nbr, ac_nbr, coupling)
    message = lax.all_to_all(message, axes, split_axis=0, concat_axis=0, tiled=True)

    x_rows = devices * count
    y_rows = devices * xs + devices // 4 * xs
    halo_shapes = [(x_rows, LANES)] * 2 + [(y_rows, LANES)] * 2
    halo_scratch = [pltpu.VMEM(shape, f32) for shape in halo_shapes]
    lamb_scratch = pltpu.VMEM((blocks, 3 * xs, LANES), f32)
    after, mean, *halos = pl.pallas_call(
        functools.partial(first_kernel, plan),
        out_shape=(
            array(f32, devices, plan.core_rows, LANES),
            array(f32, blocks, plan.core_rows, LANES),
            *(array(WIRE, *shape) for shape in halo_shapes),
        ),
        in_specs=smem(1) + vmem(1),
        out_specs=tuple(vmem(6)),
        scratch_shapes=[pltpu.VMEM((devices, plan.rows, LANES), f32), lamb_scratch] + halo_scratch,
        name="first_step",
    )(table, message)
    moves = [plan.permutation(*step) for step in ((1, 0), (-1, 0), (0, 1), (0, -1))]
    halos = [lax.ppermute(halo, axes, move) for halo, move in zip(halos, moves)]

    message = pl.pallas_call(
        functools.partial(last_kernel, plan),
        out_shape=array(WIRE, devices, plan.core_rows, LANES),
        in_specs=smem(1) + vmem(6),
        out_specs=vmem(1)[0],
        scratch_shapes=[lamb_scratch]
        + halo_scratch
        + [pltpu.VMEM((devices, plan.core_rows, LANES), f32)],
        name="last_step",
    )(table, after, mean, *halos)
    message = lax.all_to_all(message, axes, split_axis=0, concat_axis=0, tiled=True)

    result = pl.pallas_call(
        functools.partial(unpack_kernel, plan),
        out_shape=array(f32, *state.shape[2:]),
        in_specs=vmem(1),
        out_specs=vmem(1)[0],
        name="unpack",
    )(message)
    return result[None, None]


def solution(mesh):
    def program(state, mean_flow, les_owner, ac_owner, les_nbr, ac_nbr, coupling):
        plan = Plan(mesh.shape["block"], mesh.shape["section"], state.shape[2], state.shape[3])
        return jax.shard_map(
            functools.partial(on_device, plan),
            mesh=mesh,
            in_specs=(
                P("section", "block", None, None, None),
                P("block", None, None, None),
                P(),
                P(),
                P(),
                P(),
                P(),
            ),
            out_specs=P("section", "block", None, None, None),
            check_vma=False,
        )(state, mean_flow, les_owner, ac_owner, les_nbr, ac_nbr, coupling)

    return program
```

time: 742 us -> 71 us (0.10)
  the two profiles are of different devices: /device:TPU:1 before, /device:TPU:0 now
where the time goes in v1:
time: 71 us; the launch traced here: 70.6 us
  blocking collectives  45.7 us (64%)
  Pallas kernels  15.9 us (22%)
  starting transfers between devices  4.05 us (6%)
  local copies, waits for them, and re-layouts  2.71 us (4%)
  waiting for transfers between devices  2.19 us (3%)
    all_to_all x2, blocking collectives, on_device(): lax.all_to_all(message, axes, split_axis=0, concat_axis=0, tiled=True)  45.7 us
    pallas_call x1, Pallas kernels, on_device(): pl.pallas_call(functools.partial(first_kernel, plan), out_shape=(array(f3...  5.74 us
    pallas_call x1, Pallas kernels, on_device(): pl.pallas_call(functools.partial(last_kernel, plan), out_shape=array(WIRE...  4.52 us
    ppermute x4, starting transfers between devices, on_device(): halos = [lax.ppermute(halo, axes, move) for halo, move in zip(halos, moves)]  4.05 us
    pallas_call x1, Pallas kernels, on_device(): pl.pallas_call(functools.partial(pack_kernel, plan), out_shape=(array(WIR...  3.74 us
    unnamed x12, local copies, waits for them, and re-layouts  2.71 us
    ppermute x4, waiting for transfers between devices, on_device(): halos = [lax.ppermute(halo, axes, move) for halo, move in zip(halos, moves)]  2.19 us
    pallas_call x1, Pallas kernels, on_device(): pl.pallas_call(functools.partial(unpack_kernel, plan), out_shape=array(f3...  1.89 us
  transfers between devices with their start and end apart: 4, of which 1 were waited for; matrix products, arithmetic and copies ran while one was open for 0% of the time, Pallas kernels for 0%

profile of v1, /device:TPU:0, one launch (start us, length us, event | category | flops | bytes accessed | tf_op | source)
XLA Modules:
  0.0 70.6 jit_solution(9841762879255346053)
XLA Ops:
  0.0 0.0 copy-start.4
  0.0 1.4 %copy.8.les_nbr = s32[16,6]{1,0:T(8,128)} copy(s32[16,6]{0,1:T(8,128)} %param.11) | data formatting | bytes 768 | tf_op args[4]
  1.4 0.0 copy-done.4
  1.4 0.7 copy.9.ac_nbr
  2.1 3.7 %pack.1 = (s16[32,96,128]{2,1,0:T(8,128)(2,1)}, s32[224]{0:T(256)}) custom-call(f32[5,32,1024]{2,1,0:T(8,128)} %bitcast.3, f32[5,32,1024]{2,1,0:T(8,128)} %bitcast.4, s32[16]{0:T(128)} %les_owner.1, s32[16]{0:T(128)} %ac_owner.1, s32[16,6]{1,0:T(8,128)} %copy.8.les_nbr, s32[16,6]{1,0:T(8,128)} %copy.9.ac_nbr, s32[16]{0:T(128)} %coupling.1), custom_call_target="tpu_custom_call" | custom-call | tf_op jit(solution)/shard_map/pack/pallas_call | solution.py:450
  5.8 29.9 %all_to_all.10.message = s16[32,96,128]{2,1,0:T(8,128)(2,1)} all-to-all(s16[32,96,128]{2,1,0:T(8,128)(2,1)} %get-tuple-element.14), channel_id=1, replica_groups=mesh['section'=2,'block'=16] {'section','block'}, dimensions={0} | all-to-all | bytes 1572864 | tf_op jit(solution)/shard_map/all_to_all | solution.py:465
  35.7 5.7 %first_step.1 = (f32[32,40,128]{2,1,0:T(8,128)}, f32[16,40,128]{2,1,0:T(8,128)}, s16[160,128]{1,0:T(8,128)(2,1)}, s16[160,128]{1,0:T(8,128)(2,1)}, s16[320,128]{1,0:T(8,128)(2,1)}, /*index=5*/s16[320,128]{1,0:T(8,128)(2,1)}) custom-call(s32[224]{0:T(256)} %get-tuple-element.13.table, s16[32,96,128]{2,1,0:T(8,128)(2,1)} %all_to_all.10.message), custom_call_target="tpu_custom_call" | custom-call | tf_op jit(solution)/shard_map/first_step/pallas_call | solution.py:472
  41.4 0.0 collective-permute-start.2
  41.4 2.0 %collective-permute-start.3 = (s16[320,128]{1,0:T(8,128)(2,1)}, s16[320,128]{1,0:T(8,128)(2,1)S(1)}, u32[]{:S(2)}, u32[]{:S(2)}) collective-permute-start(s16[320,128]{1,0:T(8,128)(2,1)} %get-tuple-element.20), channel_id=1, source_target_pairs={{0,2},{1,3},{2,6},{3,7},{4,0},{5,1},{6,10},{7,11},{8,4},{9,5},{10,... | collective-permute-start | bytes 245768 | tf_op jit(solution)/shard_map/ppermute | solution.py:485
  43.4 0.0 collective-permute-start
  43.4 2.0 %collective-permute-start.1 = (s16[160,128]{1,0:T(8,128)(2,1)}, s16[160,128]{1,0:T(8,128)(2,1)S(1)}, u32[]{:S(2)}, u32[]{:S(2)}) collective-permute-start(s16[160,128]{1,0:T(8,128)(2,1)} %get-tuple-element.18), channel_id=1, source_target_pairs={{0,1},{1,17},{2,3},{3,19},{4,5},{5,21},{6,7},{7,23},{8,9},{9,25},{... | collective-permute-start | bytes 122888 | tf_op jit(solution)/shard_map/ppermute | solution.py:485
  45.5 2.2 %collective-permute-done.x_low = s16[160,128]{1,0:T(8,128)(2,1)S(1)} collective-permute-done((s16[160,128]{1,0:T(8,128)(2,1)}, s16[160,128]{1,0:T(8,128)(2,1)S(1)}, u32[]{:S(2)}, u32[]{:S(2)}) %collective-permute-start) | collective-permute-done | bytes 40992 | tf_op jit(solution)/shard_map/ppermute | solution.py:485
  47.6 0.0 copy-start.2
  47.6 0.0 collective-permute-done.1.x_high
  47.7 0.0 copy-start.3
  47.7 0.0 collective-permute-done.2.y_low
  47.7 0.0 copy-start
  47.7 0.0 collective-permute-done.3.y_high
  47.7 0.0 copy-start.1
  47.7 0.6 copy-done.2
  48.3 0.0 copy-done.3
  48.3 0.0 copy-done
  48.3 0.0 copy-done.1
  48.3 4.5 %last_step.1 = s16[32,40,128]{2,1,0:T(8,128)(2,1)} custom-call(s32[224]{0:T(256)} %get-tuple-element.13.table, f32[32,40,128]{2,1,0:T(8,128)} %get-tuple-element.15.before, f32[16,40,128]{2,1,0:T(8,128)} %get-tuple-element.16.mean_in, s16[160,128]{1,0:T(8,128)(2,1)} %copy-done.2, s16[160,128]{1,0:T(8,128)(2,1)} %copy-done.3, s16[320,128]{1,0:T(8,128)(2,1)} %copy-done, ...), custom_call_target="tpu_custom_call" | custom-call | tf_op jit(solution)/shard_map/last_step/pallas_call | solution.py:487
  52.9 15.9 %all_to_all.11.message = s16[32,40,128]{2,1,0:T(8,128)(2,1)} all-to-all(s16[32,40,128]{2,1,0:T(8,128)(2,1)} %last_step.1), channel_id=1, replica_groups=mesh['section'=2,'block'=16] {'section','block'}, dimensions={0} | all-to-all | bytes 655360 | tf_op jit(solution)/shard_map/all_to_all | solution.py:497
  68.7 1.9 %unpack.1 = f32[5,32,1024]{2,1,0:T(8,128)} custom-call(s16[32,40,128]{2,1,0:T(8,128)(2,1)} %all_to_all.11.message), custom_call_target="tpu_custom_call" | custom-call | tf_op jit(solution)/shard_map/unpack/pallas_call | solution.py:499
Async XLA Ops:
  0.0 1.4 %copy-start.4 = (s32[16,6]{0,1:T(8,128)S(1)}, s32[16,6]{0,1:T(8,128)}, u32[]{:S(2)}) copy-start(s32[16,6]{0,1:T(8,128)} %param.12) | copy-start | bytes 1156
  41.4 6.2 %collective-permute-start.2 = (s16[320,128]{1,0:T(8,128)(2,1)}, s16[320,128]{1,0:T(8,128)(2,1)S(1)}, u32[]{:S(2)}, u32[]{:S(2)}) collective-permute-start(s16[320,128]{1,0:T(8,128)(2,1)} %get-tuple-element.19), channel_id=1, source_target_pairs={{0,4},{1,5},{2,0},{3,1},{4,8},{5,9},{6,2},{7,3},{8,12},{9,13},{10,... | collective-permute-start | bytes 245768 | tf_op jit(solution)/shard_map/ppermute | solution.py:485
  41.4 6.3 %collective-permute-start.3 = (s16[320,128]{1,0:T(8,128)(2,1)}, s16[320,128]{1,0:T(8,128)(2,1)S(1)}, u32[]{:S(2)}, u32[]{:S(2)}) collective-permute-start(s16[320,128]{1,0:T(8,128)(2,1)} %get-tuple-element.20), channel_id=1, source_target_pairs={{0,2},{1,3},{2,6},{3,7},{4,0},{5,1},{6,10},{7,11},{8,4},{9,5},{10,... | collective-permute-start | bytes 245768 | tf_op jit(solution)/shard_map/ppermute | solution.py:485
  43.4 4.2 %collective-permute-start = (s16[160,128]{1,0:T(8,128)(2,1)}, s16[160,128]{1,0:T(8,128)(2,1)S(1)}, u32[]{:S(2)}, u32[]{:S(2)}) collective-permute-start(s16[160,128]{1,0:T(8,128)(2,1)} %get-tuple-element.17), channel_id=1, source_target_pairs={{0,16},{1,0},{2,18},{3,2},{4,20},{5,4},{6,22},{7,6},{8,24},{9,8},{... | collective-permute-start | bytes 122888 | tf_op jit(solution)/shard_map/ppermute | solution.py:485
  43.4 4.2 %collective-permute-start.1 = (s16[160,128]{1,0:T(8,128)(2,1)}, s16[160,128]{1,0:T(8,128)(2,1)S(1)}, u32[]{:S(2)}, u32[]{:S(2)}) collective-permute-start(s16[160,128]{1,0:T(8,128)(2,1)} %get-tuple-element.18), channel_id=1, source_target_pairs={{0,1},{1,17},{2,3},{3,19},{4,5},{5,21},{6,7},{7,23},{8,9},{9,25},{... | collective-permute-start | bytes 122888 | tf_op jit(solution)/shard_map/ppermute | solution.py:485
  47.6 0.6 copy-start.2
  47.7 0.6 copy-start.3
  47.7 0.7 copy-start
  47.7 0.7 copy-start.1

commit v2 on v1

--- a/solution.py
+++ b/solution.py
@@ -79,7 +79,8 @@
 
 
 def roll_lanes(tile, shift):
-    return pltpu.roll(tile, shift % LANES, 1)
+    shift = shift % LANES
+    return pltpu.roll(tile, shift, 1) if shift else tile
 
 
 def roll_rows(tile, shift):
@@ -95,16 +96,37 @@
 
 
 def pack_kernel(
-    plan, state, mean, les_owner, ac_owner, les_nbr, ac_nbr, coupling,
-    message, table, raw, filled, les_inv, ac_inv, pair_inv,
+    plan, state_hbm, mean_hbm, *refs
 ):
+    lookups_hbm, (message, table), rest = refs[:5], refs[5:7], refs[7:]
+    lookups, rest = rest[:5], rest[5:]
+    state, mean, filled, les_inv, ac_inv, pair_inv, small_sem, state_sem, mean_sem = rest
+    les_owner, ac_owner, les_nbr, ac_nbr, coupling = lookups
+    small = [
+        pltpu.make_async_copy(source, target, small_sem.at[i])
+        for i, (source, target) in enumerate(zip(lookups_hbm, lookups))
+    ]
+    for copy in small:
+        copy.start()
+    large = []
+    for v in range(plan.vars):
+        large.append(pltpu.make_async_copy(state_hbm.at[v], state.at[v], state_sem.at[v]))
+        large.append(pltpu.make_async_copy(mean_hbm.at[v], mean.at[v], mean_sem.at[v]))
+    for copy in large:
+        copy.start()
     section = lax.axis_index("section")
     px, py = plan.own_piece(section, lax.axis_index("block"))
+    for copy in small:
+        copy.wait()
+    look_up(plan, px, py, table, lookups, les_inv, ac_inv, pair_inv)
+    for copy in large:
+        copy.wait()
+
     xs, side, half = plan.xs, plan.side, plan.half
     width = side * side
+    offsets = [jnp.where(section == 0, OFFSETS[0][v], OFFSETS[1][v]) for v in range(plan.vars)]
     for v in range(plan.vars):
-        offset = jnp.where(section == 0, OFFSETS[0][v], OFFSETS[1][v])
-        raw[v] = (state[v] - offset) * SCALE_IN
+        state[v] = (state[v] - offsets[v]) * SCALE_IN
     lane = lane_index(xs)
     for device in range(plan.devices):
         tx, ty = plan.piece(device)
@@ -113,53 +135,59 @@
         before = (l0 - LANES) % width
         after = (l0 + LANES) % width
         for v in range(plan.vars):
-            filled[device, v * xs : (v + 1) * xs, :] = raw[v, x0 : x0 + xs, here]
-            filled[device, plan.x_base + v, :] = raw[v, (x0 - 1) % side, here]
-            filled[device, plan.x_base + plan.vars + v, :] = raw[v, (x0 + xs) % side, here]
+            filled[device, v * xs : (v + 1) * xs, :] = state[v, x0 : x0 + xs, here]
+            filled[device, plan.x_base + v, :] = state[v, (x0 - 1) % side, here]
+            filled[device, plan.x_base + plan.vars + v, :] = state[v, (x0 + xs) % side, here]
             first, second = mean[v, x0 : x0 + half, here], mean[v, x0 + half : x0 + xs, here]
             piece = jnp.where(section == 0, first, second)
             base = plan.mean_base + v * half
             filled[device, base : base + half, :] = (piece - MEAN_OFFSETS[v]) * SCALE_IN
         for i, (a, b) in enumerate(PAIRS):
-            low_a = raw[a, x0 : x0 + xs, before : before + LANES]
-            low_b = raw[b, x0 : x0 + xs, before : before + LANES]
-            high_a = raw[a, x0 : x0 + xs, after : after + LANES]
-            high_b = raw[b, x0 : x0 + xs, after : after + LANES]
-            low = jnp.where(lane < side, roll_lanes(low_a, side), roll_lanes(high_b, side))
-            high = jnp.where(lane < 3 * side, roll_lanes(low_b, -side), roll_lanes(high_a, -side))
+            edge = [
+                jnp.where(
+                    lane >= LANES - side,
+                    state[v, x0 : x0 + xs, before : before + LANES],
+                    state[v, x0 : x0 + xs, after : after + LANES],
+                )
+                for v in ((a, b) if a != b else (a,))
+            ]
+            tile = edge[0]
+            if a != b:
+                outer = (lane < side) | (lane >= LANES - side)
+                tile = jnp.where(outer, edge[0], roll_lanes(edge[1], LANES // 2))
             base = plan.y_base + i * xs
-            filled[device, base : base + xs, :] = jnp.where(lane < 2 * side, low, high)
+            filled[device, base : base + xs, :] = tile
         used = plan.x_base + 2 * plan.vars
         if used < plan.rows:
             filled[device, used:, :] = jnp.zeros((plan.rows - used, LANES), jnp.float32)
         message[device] = to_wire(filled[device])
 
-    def invert(i, carry):
+
+def look_up(plan, px, py, table, lookups, les_inv, ac_inv, pair_inv):
+    les_owner, ac_owner, les_nbr, ac_nbr, coupling = lookups
+    for i in range(plan.blocks):
         les_inv[les_owner[i]] = i
         ac_inv[ac_owner[i]] = i
         pair_inv[coupling[i]] = i
-        return carry
-
-    lax.fori_loop(0, plan.blocks, invert, 0)
     at_edge = (px == 0, px == plan.nx - 1, py == 0, py == plan.ny - 1, True, True)
-
-    def look_up(slot, carry):
+    faces = FACES if plan.layers_z > 1 else 4
+    for slot in range(plan.blocks):
         les_block = les_inv[slot]
         ac_block = ac_inv[slot]
         for kind, (block, nbr, owner) in enumerate(
             ((les_block, les_nbr, les_owner), (ac_block, ac_nbr, ac_owner))
         ):
             for face in range(FACES):
-                other = nbr[block, face]
-                source = jnp.where(other < 0, -1, owner[jnp.maximum(other, 0)])
-                if face < 4:
-                    source = jnp.where(at_edge[face], source, slot)
+                if face < faces:
+                    other = nbr[face, block]
+                    source = jnp.where(other < 0, -1, owner[jnp.maximum(other, 0)])
+                    if face < 4:
+                        source = jnp.where(at_edge[face], source, slot)
+                else:
+                    source = -1
                 table[(kind * COLUMNS + face) * plan.blocks + slot] = source
         table[FACES * plan.blocks + slot] = ac_owner[pair_inv[les_block]]
         table[(COLUMNS + FACES) * plan.blocks + slot] = les_owner[coupling[ac_block]]
-        return carry
-
-    lax.fori_loop(0, plan.blocks, look_up, 0)
 
 
 def sides(plan, table, kind, slot, core, x_halo, y_halo):
@@ -167,20 +195,21 @@
     lane = lane_index(xs)
     row = lax.broadcasted_iota(jnp.int32, (xs, LANES), 0)
     depth = lane % side
-    found = [table[(kind * COLUMNS + face) * plan.blocks + slot] for face in range(FACES)]
+    faces = FACES if plan.layers_z > 1 else 4
+    found = [table[(kind * COLUMNS + face) * plan.blocks + slot] for face in range(faces)]
     inside = [f >= 0 for f in found]
     found = [jnp.maximum(f, 0) for f in found]
     own = [core(kind, slot, v) for v in range(plan.vars)]
     shifted = [[] for _ in range(FACES)]
     for v, tile in enumerate(own):
-        low = jnp.where(inside[0], x_halo(kind, found[0], v, 0), tile[0:1])
-        high = jnp.where(inside[1], x_halo(kind, found[1], v, 1), tile[xs - 1 : xs])
+        low = jnp.where(inside[0], x_halo(kind, found[0], v, 0), tile)
+        high = jnp.where(inside[1], x_halo(kind, found[1], v, 1), tile)
         shifted[0].append(jnp.where(row == 0, low, roll_rows(tile, 1)))
         shifted[1].append(jnp.where(row == xs - 1, high, roll_rows(tile, -1)))
-        low = jnp.where(inside[2], y_halo(kind, found[2], v, 0), tile)
-        high = jnp.where(inside[3], y_halo(kind, found[3], v, 1), tile)
-        shifted[2].append(jnp.where(lane < side, low, roll_lanes(tile, side)))
-        shifted[3].append(jnp.where(lane >= LANES - side, high, roll_lanes(tile, -side)))
+        low = roll_lanes(jnp.where(lane >= LANES - side, y_halo(kind, found[2], v, 0), tile), side)
+        high = roll_lanes(jnp.where(lane < side, y_halo(kind, found[3], v, 1), tile), -side)
+        shifted[2].append(jnp.where((lane < side) & ~inside[2], tile, low))
+        shifted[3].append(jnp.where((lane >= LANES - side) & ~inside[3], tile, high))
         low, high = tile, tile
         if plan.layers_z > 1:
             low = jnp.where(inside[4], roll_lanes(core(kind, found[4], v), 1 - side), tile)
@@ -282,8 +311,8 @@
         store(1, slot, ac_slot(plan, own, shifted, mean(slot), source))
         return carry
 
-    lax.fori_loop(0, plan.blocks, les_body, 0, unroll=2)
-    lax.fori_loop(0, plan.blocks, ac_body, 0, unroll=2)
+    lax.fori_loop(0, plan.blocks, les_body, 0, unroll=4)
+    lax.fori_loop(0, plan.blocks, ac_body, 0, unroll=4)
 
 
 def tile_rows(plan, v):
@@ -329,7 +358,7 @@
         base = plan.y_base + (v // 2) * xs
         tile = arrived[kind * blocks + slot, base : base + xs, :]
         if v % 2 == 1:
-            tile = roll_lanes(tile, 2 * side)
+            tile = roll_lanes(tile, LANES // 2)
         return shift_back(tile, kind, v)
 
     def mean(slot):
@@ -387,12 +416,13 @@
 
     def x_halo(kind, slot, v, end):
         raw = x_high_raw if end else x_low_raw
-        return shift_back(raw[pl.ds((kind * blocks + slot) * count + v, 1), :], kind, v)
+        at = (kind * blocks + slot) * count + v
+        return shift_back(raw[pl.ds(at, 1), :], kind, v)
 
     def y_halo(kind, slot, v, end):
         raw = y_high_raw if end else y_low_raw
         m = kind * blocks + slot
-        target = 3 * side if end else 0
+        target = 0 if end else 3 * side
         if v < 4:
             tile = raw[pl.ds(pl.multiple_of(m * xs, xs), xs), :]
             tile = roll_lanes(tile, target - side * v)
@@ -447,21 +477,27 @@
     def array(dtype, *shape):
         return jax.ShapeDtypeStruct(shape, dtype)
 
+    far = [
+        pltpu.with_memory_space_constraint(a, pltpu.HBM)
+        for a in (state[0, 0], mean_flow[0], les_owner, ac_owner, les_nbr.T, ac_nbr.T, coupling)
+    ]
+    volume = pltpu.VMEM((count, plan.side, plan.side * plan.side), f32)
+    lookups = [pltpu.SMEM(a.shape, jnp.int32) for a in far[2:]]
     message, table = pl.pallas_call(
         functools.partial(pack_kernel, plan),
         out_shape=(
             array(WIRE, devices, plan.rows, LANES),
             array(jnp.int32, 2 * COLUMNS * blocks),
         ),
-        in_specs=vmem(2) + smem(5),
+        in_specs=[pl.BlockSpec(memory_space=pltpu.HBM)] * len(far),
         out_specs=tuple(vmem(1) + smem(1)),
-        scratch_shapes=[
-            pltpu.VMEM((count, plan.side, plan.side * plan.side), f32),
-            pltpu.VMEM((devices, plan.rows, LANES), f32),
-        ]
-        + [pltpu.SMEM((blocks,), jnp.int32)] * 3,
+        scratch_shapes=lookups
+        + [volume, volume, pltpu.VMEM((devices, plan.rows, LANES), f32)]
+        + [pltpu.SMEM((blocks,), jnp.int32)] * 3
+        + [pltpu.SemaphoreType.DMA((n,)) for n in (len(lookups), count, count)],
         name="pack",
-    )(state[0, 0], mean_flow[0], les_owner, ac_owner, les_nbr, ac_nbr, coupling)
+        compiler_params=pltpu.CompilerParams(vmem_limit_bytes=16 * 1024 * 1024),
+    )(*far)
     message = lax.all_to_all(message, axes, split_axis=0, concat_axis=0, tiled=True)
 
     x_rows = devices * count
@@ -480,6 +516,7 @@
         out_specs=tuple(vmem(6)),
         scratch_shapes=[pltpu.VMEM((devices, plan.rows, LANES), f32), lamb_scratch] + halo_scratch,
         name="first_step",
+        compiler_params=pltpu.CompilerParams(vmem_limit_bytes=16 * 1024 * 1024),
     )(table, message)
     moves = [plan.permutation(*step) for step in ((1, 0), (-1, 0), (0, 1), (0, -1))]
     halos = [lax.ppermute(halo, axes, move) for halo, move in zip(halos, moves)]
@@ -493,6 +530,7 @@
         + halo_scratch
         + [pltpu.VMEM((devices, plan.core_rows, LANES), f32)],
         name="last_step",
+        compiler_params=pltpu.CompilerParams(vmem_limit_bytes=16 * 1024 * 1024),
     )(table, after, mean, *halos)
     message = lax.all_to_all(message, axes, split_axis=0, concat_axis=0, tiled=True)
 
@@ -502,6 +540,7 @@
         in_specs=vmem(1),
         out_specs=vmem(1)[0],
         name="unpack",
+        compiler_params=pltpu.CompilerParams(vmem_limit_bytes=16 * 1024 * 1024),
     )(message)
     return result[None, None]
 

time: 71 us -> 60.4 us (0.85)
  Pallas kernels: 15.9 us -> 9.45 us
  local copies, waits for them, and re-layouts: 2.71 us -> 0 us
  blocking collectives: 45.7 us -> 44.6 us
    unnamed x12 -> x0, local copies, waits for them, and re-layouts: 2.71 us -> none
    pallas_call x1, Pallas kernels: 5.74 us -> 3.32 us  [on_device(): pl.pallas_call(functools.partial(first_kernel, plan), out_shape=(array(f3...]
    pallas_call x1, Pallas kernels: 4.52 us -> 2.86 us  [on_device(): pl.pallas_call(functools.partial(last_kernel, plan), out_shape=array(WIRE...]
    pallas_call x1, Pallas kernels: 3.74 us -> 2.34 us  [on_device(): pl.pallas_call(functools.partial(pack_kernel, plan), out_shape=(array(WIR...]
    all_to_all x2, blocking collectives: 45.7 us -> 44.6 us  [on_device(): lax.all_to_all(message, axes, split_axis=0, concat_axis=0, tiled=True)]
    pallas_call x1, Pallas kernels: 1.89 us -> 0.92 us  [on_device(): pl.pallas_call(functools.partial(unpack_kernel, plan), out_shape=array(f3...]
where the time goes in v2:
time: 60.4 us; the launch traced here: 60.2 us
  blocking collectives  44.6 us (74%)
  Pallas kernels  9.45 us (16%)
  starting transfers between devices  4.1 us (7%)
  waiting for transfers between devices  1.98 us (3%)
    all_to_all x2, blocking collectives, on_device(): lax.all_to_all(message, axes, split_axis=0, concat_axis=0, tiled=True)  44.6 us
    ppermute x4, starting transfers between devices, on_device(): halos = [lax.ppermute(halo, axes, move) for halo, move in zip(halos, moves)]  4.1 us
    pallas_call x1, Pallas kernels, on_device(): pl.pallas_call(functools.partial(first_kernel, plan), out_shape=(array(f3...  3.32 us
    pallas_call x1, Pallas kernels, on_device(): pl.pallas_call(functools.partial(last_kernel, plan), out_shape=array(WIRE...  2.86 us
    pallas_call x1, Pallas kernels, on_device(): pl.pallas_call(functools.partial(pack_kernel, plan), out_shape=(array(WIR...  2.34 us
    ppermute x4, waiting for transfers between devices, on_device(): halos = [lax.ppermute(halo, axes, move) for halo, move in zip(halos, moves)]  1.98 us
  transfers between devices with their start and end apart: 4, of which 1 were waited for; matrix products, arithmetic and copies ran while one was open for 0% of the time, Pallas kernels for 0%

profile of v2, /device:TPU:0, one launch (start us, length us, event | category | flops | bytes accessed | tf_op | source)
XLA Modules:
  0.0 60.2 jit_solution(12425475169678092281)
XLA Ops:
  0.0 2.3 %pack.1 = (s16[32,96,128]{2,1,0:T(8,128)(2,1)S(1)}, s32[224]{0:T(256)S(1)}) custom-call(f32[5,32,1024]{2,1,0:T(8,128)} %bitcast.5, f32[5,32,1024]{2,1,0:T(8,128)} %bitcast.6, s32[16]{0:T(128)} %refs_0_.1, s32[16]{0:T(128)} %refs_1_.1, s32[6,16]{1,0:T(8,128)} %bitcast.7, s32[6,16]{1,0:T(8,128)} %bitcast.8, s32[16]{0:T(128)} %refs_4_.1), custom_call_target="tpu_custom_call" | custom-call | tf_op jit(solution)/shard_map/pack/pallas_call | solution.py:486
  2.4 29.6 %all_to_all.10.message = s16[32,96,128]{2,1,0:T(8,128)(2,1)S(1)} all-to-all(s16[32,96,128]{2,1,0:T(8,128)(2,1)S(1)} %get-tuple-element.14), channel_id=1, replica_groups=mesh['section'=2,'block'=16] {'section','block'}, dimensions={0} | all-to-all | bytes 1572864 | tf_op jit(solution)/shard_map/all_to_all | solution.py:501
  31.9 3.3 %first_step.1 = (f32[32,40,128]{2,1,0:T(8,128)S(1)}, f32[16,40,128]{2,1,0:T(8,128)S(1)}, s16[160,128]{1,0:T(8,128)(2,1)S(1)}, s16[160,128]{1,0:T(8,128)(2,1)S(1)...) custom-call(s32[224]{0:T(256)S(1)} %get-tuple-element.13.table, s16[32,96,128]{2,1,0:T(8,128)(2,1)S(1)} %all_to_all.10.message), custom_call_target="tpu_custom_call" | custom-call | tf_op jit(solution)/shard_map/first_step/pallas_call | solution.py:508
  35.2 0.1 collective-permute-start.2
  35.3 2.0 %collective-permute-start.3 = (s16[320,128]{1,0:T(8,128)(2,1)S(1)}, s16[320,128]{1,0:T(8,128)(2,1)S(1)}, u32[]{:S(2)}, u32[]{:S(2)}) collective-permute-start(s16[320,128]{1,0:T(8,128)(2,1)S(1)} %get-tuple-element.20), channel_id=1, source_target_pairs={{0,2},{1,3},{2,6},{3,7},{4,0},{5,1},{6,10},{7,11},{8,4},{9,5},{10,... | collective-permute-start | bytes 245768 | tf_op jit(solution)/shard_map/ppermute | solution.py:522
  37.3 0.0 collective-permute-start
  37.3 2.0 %collective-permute-start.1 = (s16[160,128]{1,0:T(8,128)(2,1)S(1)}, s16[160,128]{1,0:T(8,128)(2,1)S(1)}, u32[]{:S(2)}, u32[]{:S(2)}) collective-permute-start(s16[160,128]{1,0:T(8,128)(2,1)S(1)} %get-tuple-element.18), channel_id=1, source_target_pairs={{0,1},{1,17},{2,3},{3,19},{4,5},{5,21},{6,7},{7,23},{8,9},{9,25},{... | collective-permute-start | bytes 122888 | tf_op jit(solution)/shard_map/ppermute | solution.py:522
  39.3 2.0 %collective-permute-done.x_low = s16[160,128]{1,0:T(8,128)(2,1)S(1)} collective-permute-done((s16[160,128]{1,0:T(8,128)(2,1)S(1)}, s16[160,128]{1,0:T(8,128)(2,1)S(1)}, u32[]{:S(2)}, u32[]{:S(2)}) %collective-permute-start) | collective-permute-done | bytes 40992 | tf_op jit(solution)/shard_map/ppermute | solution.py:522
  41.3 0.0 collective-permute-done.1.x_high
  41.3 0.0 collective-permute-done.2.y_low
  41.3 0.0 collective-permute-done.3.y_high
  41.3 2.9 %last_step.1 = s16[32,40,128]{2,1,0:T(8,128)(2,1)S(1)} custom-call(s32[224]{0:T(256)S(1)} %get-tuple-element.13.table, f32[32,40,128]{2,1,0:T(8,128)S(1)} %get-tuple-element.15.before, f32[16,40,128]{2,1,0:T(8,128)S(1)} %get-tuple-element.16.mean_in, s16[160,128]{1,0:T(8,128)(2,1)S(1)} %collective-permute-done.x_low, ...), custom_call_target="tpu_custom_call" | custom-call | tf_op jit(solution)/shard_map/last_step/pallas_call | solution.py:524
  44.2 15.1 %all_to_all.11.message = s16[32,40,128]{2,1,0:T(8,128)(2,1)S(1)} all-to-all(s16[32,40,128]{2,1,0:T(8,128)(2,1)S(1)} %last_step.1), channel_id=1, replica_groups=mesh['section'=2,'block'=16] {'section','block'}, dimensions={0} | all-to-all | bytes 655360 | tf_op jit(solution)/shard_map/all_to_all | solution.py:535
  59.3 0.9 %unpack.1 = f32[5,32,1024]{2,1,0:T(8,128)} custom-call(s16[32,40,128]{2,1,0:T(8,128)(2,1)S(1)} %all_to_all.11.message), custom_call_target="tpu_custom_call" | custom-call | tf_op jit(solution)/shard_map/unpack/pallas_call | solution.py:537
Async XLA Ops:
  35.2 6.1 %collective-permute-start.2 = (s16[320,128]{1,0:T(8,128)(2,1)S(1)}, s16[320,128]{1,0:T(8,128)(2,1)S(1)}, u32[]{:S(2)}, u32[]{:S(2)}) collective-permute-start(s16[320,128]{1,0:T(8,128)(2,1)S(1)} %get-tuple-element.19), channel_id=1, source_target_pairs={{0,4},{1,5},{2,0},{3,1},{4,8},{5,9},{6,2},{7,3},{8,12},{9,13},{10,... | collective-permute-start | bytes 245768 | tf_op jit(solution)/shard_map/ppermute | solution.py:522
  35.3 6.0 %collective-permute-start.3 = (s16[320,128]{1,0:T(8,128)(2,1)S(1)}, s16[320,128]{1,0:T(8,128)(2,1)S(1)}, u32[]{:S(2)}, u32[]{:S(2)}) collective-permute-start(s16[320,128]{1,0:T(8,128)(2,1)S(1)} %get-tuple-element.20), channel_id=1, source_target_pairs={{0,2},{1,3},{2,6},{3,7},{4,0},{5,1},{6,10},{7,11},{8,4},{9,5},{10,... | collective-permute-start | bytes 245768 | tf_op jit(solution)/shard_map/ppermute | solution.py:522
  37.3 4.0 %collective-permute-start = (s16[160,128]{1,0:T(8,128)(2,1)S(1)}, s16[160,128]{1,0:T(8,128)(2,1)S(1)}, u32[]{:S(2)}, u32[]{:S(2)}) collective-permute-start(s16[160,128]{1,0:T(8,128)(2,1)S(1)} %get-tuple-element.17), channel_id=1, source_target_pairs={{0,16},{1,0},{2,18},{3,2},{4,20},{5,4},{6,22},{7,6},{8,24},{9,8},{... | collective-permute-start | bytes 122888 | tf_op jit(solution)/shard_map/ppermute | solution.py:522
  37.3 4.0 %collective-permute-start.1 = (s16[160,128]{1,0:T(8,128)(2,1)S(1)}, s16[160,128]{1,0:T(8,128)(2,1)S(1)}, u32[]{:S(2)}, u32[]{:S(2)}) collective-permute-start(s16[160,128]{1,0:T(8,128)(2,1)S(1)} %get-tuple-element.18), channel_id=1, source_target_pairs={{0,1},{1,17},{2,3},{3,19},{4,5},{5,21},{6,7},{7,23},{8,9},{9,25},{... | collective-permute-start | bytes 122888 | tf_op jit(solution)/shard_map/ppermute | solution.py:522

commit v3 on v2

--- a/solution.py
+++ b/solution.py
@@ -17,7 +17,7 @@
 FEEDBACK_GAIN = 0.5
 
 WIRE = jnp.int16
-SCALE_IN = 32000.0
+SCALE_IN = 16384.0
 SCALE_MID = 8192.0
 SCALE_OUT = 4096.0
 OFFSETS = ((1.25, 0.0, 0.0, 0.0, 2.6), (0.0, 0.0, 0.0, 0.0, 0.0))
@@ -190,17 +190,14 @@
         table[(COLUMNS + FACES) * plan.blocks + slot] = les_owner[coupling[ac_block]]
 
 
-def sides(plan, table, kind, slot, core, x_halo, y_halo):
+def sides_xy(plan, table, kind, slot, own, x_halo, y_halo):
     xs, side = plan.xs, plan.side
     lane = lane_index(xs)
     row = lax.broadcasted_iota(jnp.int32, (xs, LANES), 0)
-    depth = lane % side
-    faces = FACES if plan.layers_z > 1 else 4
-    found = [table[(kind * COLUMNS + face) * plan.blocks + slot] for face in range(faces)]
+    found = [table[(kind * COLUMNS + face) * plan.blocks + slot] for face in range(4)]
     inside = [f >= 0 for f in found]
     found = [jnp.maximum(f, 0) for f in found]
-    own = [core(kind, slot, v) for v in range(plan.vars)]
-    shifted = [[] for _ in range(FACES)]
+    shifted = [[] for _ in range(4)]
     for v, tile in enumerate(own):
         low = jnp.where(inside[0], x_halo(kind, found[0], v, 0), tile)
         high = jnp.where(inside[1], x_halo(kind, found[1], v, 1), tile)
@@ -210,13 +207,25 @@
         high = roll_lanes(jnp.where(lane < side, y_halo(kind, found[3], v, 1), tile), -side)
         shifted[2].append(jnp.where((lane < side) & ~inside[2], tile, low))
         shifted[3].append(jnp.where((lane >= LANES - side) & ~inside[3], tile, high))
+    return shifted
+
+
+def sides_z(plan, table, kind, slot, own, core):
+    side = plan.side
+    depth = lane_index(plan.xs) % side
+    shifted = [[], []]
+    if plan.layers_z > 1:
+        found = [table[(kind * COLUMNS + face) * plan.blocks + slot] for face in (4, 5)]
+        inside = [f >= 0 for f in found]
+        found = [jnp.maximum(f, 0) for f in found]
+    for v, tile in enumerate(own):
         low, high = tile, tile
         if plan.layers_z > 1:
-            low = jnp.where(inside[4], roll_lanes(core(kind, found[4], v), 1 - side), tile)
-            high = jnp.where(inside[5], roll_lanes(core(kind, found[5], v), side - 1), tile)
-        shifted[4].append(jnp.where(depth == 0, low, roll_lanes(tile, 1)))
-        shifted[5].append(jnp.where(depth == side - 1, high, roll_lanes(tile, -1)))
-    return own, shifted
+            low = jnp.where(inside[0], roll_lanes(core(kind, found[0], v), 1 - side), tile)
+            high = jnp.where(inside[1], roll_lanes(core(kind, found[1], v), side - 1), tile)
+        shifted[0].append(jnp.where(depth == 0, low, roll_lanes(tile, 1)))
+        shifted[1].append(jnp.where(depth == side - 1, high, roll_lanes(tile, -1)))
+    return shifted
 
 
 def primitives(conserved):
@@ -251,68 +260,99 @@
     return tile.astype(jnp.bfloat16).astype(jnp.float32)
 
 
-def les_slot(plan, own, shifted):
-    count = plan.vars
-    total = [(1.0 - 6.0 * DT_LES * VISCOSITY) * own[v] for v in range(count)]
+def plus(total, term):
+    return term if total is None else total + term
+
+
+def les_axes(plan, total, axes, pairs):
+    nearby, outflow = [None] * plan.vars, [None] * plan.vars
     gradient = []
-    for axis in range(3):
-        low, high = shifted[2 * axis], shifted[2 * axis + 1]
+    for axis, (low, high) in zip(axes, pairs):
         flux_low, speed_low = flux_along(low, axis)
         flux_high, speed_high = flux_along(high, axis)
-        for v in range(count):
-            total[v] = total[v] + (
-                DT_LES * VISCOSITY * (low[v] + high[v]) - 0.5 * DT_LES * (flux_high[v] - flux_low[v])
-            )
-        gradient.append([0.5 * (h - w) for h, w in zip(speed_high, speed_low)])
-    velocity = [m * (1.0 / own[0]) for m in own[1:4]]
-    vorticity = [
-        gradient[1][2] - gradient[2][1],
-        gradient[2][0] - gradient[0][2],
-        gradient[0][1] - gradient[1][0],
-    ]
+        for v in range(plan.vars):
+            nearby[v] = plus(nearby[v], low[v] + high[v])
+            outflow[v] = plus(outflow[v], flux_high[v] - flux_low[v])
+        gradient.append([h - w for h, w in zip(speed_high, speed_low)])
+    near, out = 0.5 * DT_LES * VISCOSITY, 0.25 * DT_LES
+    return [t + (near * n - out * o) for t, n, o in zip(total, nearby, outflow)], gradient
+
+
+def les_z(plan, table, slot, core, unit):
+    own = [core(0, slot, v) for v in range(plan.vars)]
+    total = [(0.5 - 3.0 * DT_LES * VISCOSITY) * g for g in own]
+    total, gradient = les_axes(plan, total, (2,), [sides_z(plan, table, 0, slot, own, core)])
+    partner = table[FACES * plan.blocks + slot]
+    for j in range(3):
+        back = as_bf16(core(1, partner, 1 + j))
+        total[1 + j] = total[1 + j] + (0.5 * DT_LES * FEEDBACK_GAIN) * back
+    inverse = unit / own[0]
+    return total + gradient[0][:2] + [m * inverse for m in own[1:4]]
+
+
+def les_xy(plan, part, shifted):
+    count = plan.vars
+    pairs = [shifted[0:2], shifted[2:4]]
+    total, (along_x, along_y) = les_axes(plan, part[:count], (0, 1), pairs)
+    along_z, velocity = part[count : count + 2], part[count + 2 :]
+    vorticity = [along_y[2] - along_z[1], along_z[0] - along_x[2], along_x[1] - along_y[0]]
     return total, [as_bf16(t) for t in cross(vorticity, velocity)]
 
 
-def ac_slot(plan, own, shifted, mean, source):
-    slope = [
-        [0.5 * (h - w) for h, w in zip(shifted[2 * axis + 1], shifted[2 * axis])] for axis in range(3)
-    ]
-    carried = [
-        mean[1] * slope[0][v] + mean[2] * slope[1][v] + mean[3] * slope[2][v]
-        for v in range(plan.vars)
-    ]
-    divergence = slope[0][1] + slope[1][2] + slope[2][3]
+def ac_axes(plan, total, axes, pairs, mean, source):
+    slope = [[h - w for h, w in zip(high, low)] for low, high in pairs]
+    change = [None] * plan.vars
+    divergence = None
+    for axis, s in zip(axes, slope):
+        change = [plus(c, mean[1 + axis] * t) for c, t in zip(change, s)]
+        divergence = plus(divergence, s[1 + axis])
     inverse = 1.0 / mean[0]
-    change = [carried[0] + mean[0] * divergence]
-    for axis in range(3):
-        change.append(carried[1 + axis] + slope[axis][4] * inverse + source[axis])
-    change.append(carried[4] + 1.4 * mean[4] * divergence)
-    return [g - DT_AC * c for g, c in zip(own, change)]
-
-
-def advance(plan, table, core, x_halo, y_halo, mean, lamb, store):
+    for axis, s in zip(axes, slope):
+        change[1 + axis] = change[1 + axis] + s[4] * inverse
+    if source is not None:
+        change[1:4] = [c + t for c, t in zip(change[1:4], source)]
+    change[0] = change[0] + mean[0] * divergence
+    change[4] = change[4] + 1.4 * mean[4] * divergence
+    return [t - (0.25 * DT_AC) * c for t, c in zip(total, change)]
+
+
+def ac_z(plan, table, slot, core, mean):
+    own = [core(1, slot, v) for v in range(plan.vars)]
+    pair = sides_z(plan, table, 1, slot, own, core)
+    return ac_axes(plan, [0.5 * g for g in own], (2,), [pair], mean(slot), None)
+
+
+def advance(plan, table, core, x_halo, y_halo, mean, lamb, les_part, ac_part, store):
     xs = plan.xs
 
-    def les_body(slot, carry):
-        own, shifted = sides(plan, table, 0, slot, core, x_halo, y_halo)
-        total, vector = les_slot(plan, own, shifted)
-        partner = table[FACES * plan.blocks + slot]
-        for j in range(3):
-            back = as_bf16(core(1, partner, 1 + j))
-            total[1 + j] = total[1 + j] + DT_LES * FEEDBACK_GAIN * back
-            lamb[slot, j * xs : (j + 1) * xs, :] = vector[j]
-        store(0, slot, total)
+    def les_quad(quad, carry):
+        results = []
+        for r in range(4):
+            slot = quad * 4 + r
+            own = [core(0, slot, v) for v in range(plan.vars)]
+            shifted = sides_xy(plan, table, 0, slot, own, x_halo, y_halo)
+            total, vector = les_xy(plan, les_part(slot), shifted)
+            for j in range(3):
+                lamb[slot, j * xs : (j + 1) * xs, :] = vector[j]
+            results.append(total)
+        store(0, quad, results)
         return carry
 
-    def ac_body(slot, carry):
-        own, shifted = sides(plan, table, 1, slot, core, x_halo, y_halo)
-        partner = table[(COLUMNS + FACES) * plan.blocks + slot]
-        source = [lamb[partner, j * xs : (j + 1) * xs, :] for j in range(3)]
-        store(1, slot, ac_slot(plan, own, shifted, mean(slot), source))
+    def ac_quad(quad, carry):
+        results = []
+        for r in range(4):
+            slot = quad * 4 + r
+            own = [core(1, slot, v) for v in range(plan.vars)]
+            shifted = sides_xy(plan, table, 1, slot, own, x_halo, y_halo)
+            partner = table[(COLUMNS + FACES) * plan.blocks + slot]
+            source = [lamb[partner, j * xs : (j + 1) * xs, :] for j in range(3)]
+            pairs = [shifted[0:2], shifted[2:4]]
+            results.append(ac_axes(plan, ac_part(slot), (0, 1), pairs, mean(slot), source))
+        store(1, quad, results)
         return carry
 
-    lax.fori_loop(0, plan.blocks, les_body, 0, unroll=4)
-    lax.fori_loop(0, plan.blocks, ac_body, 0, unroll=4)
+    lax.fori_loop(0, plan.blocks // 4, les_quad, 0)
+    lax.fori_loop(0, plan.blocks // 4, ac_quad, 0)
 
 
 def tile_rows(plan, v):
@@ -322,16 +362,33 @@
 def first_kernel(
     plan, table, message,
     after, mean_out, x_up, x_down, y_up, y_down,
-    arrived, lamb, x_up_raw, x_down_raw, y_up_raw, y_down_raw,
+    arrived, origin, lamb, x_up_raw, x_down_raw, y_up_raw, y_down_raw,
 ):
     xs, side, count, blocks, half = plan.xs, plan.side, plan.vars, plan.blocks, plan.half
     lane = lane_index(xs)
-
-    def read(m, carry):
-        arrived[m] = from_wire(message[m]) * (1.0 / SCALE_IN)
+    outer = (lane < side) | (lane >= LANES - side)
+
+    for kind in range(2):
+        origin[kind] = jnp.zeros((plan.rows, LANES), jnp.float32)
+        for v, offset in enumerate(MEAN_OFFSETS):
+            base = plan.mean_base + v * half
+            origin[kind, base : base + half, :] = jnp.full((half, LANES), offset * SCALE_IN, jnp.float32)
+        for v, offset in enumerate(OFFSETS[kind]):
+            if offset == 0.0:
+                continue
+            level = jnp.full((xs, LANES), offset * SCALE_IN, jnp.float32)
+            origin[kind, tile_rows(plan, v), :] = level
+            for end in range(2):
+                origin[kind, plan.x_base + end * count + v, :] = level[0]
+            base = plan.y_base + (v // 2) * xs
+            origin[kind, base : base + xs, :] = jnp.where(outer, level, 0.0)
+
+    def read(slot, carry):
+        for kind in range(2):
+            arrived[kind * blocks + slot] = from_wire(message[kind * blocks + slot]) + origin[kind]
         return carry
 
-    lax.fori_loop(0, plan.devices, read, 0, unroll=2)
+    lax.fori_loop(0, blocks, read, 0, unroll=2)
 
     def read_mean(slot, carry):
         for v in range(count):
@@ -339,77 +396,96 @@
             for part in range(plan.devices // blocks):
                 rows = arrived[part * blocks + slot, base : base + half, :]
                 start = v * xs + part * half
-                mean_out[slot, start : start + half, :] = rows + MEAN_OFFSETS[v]
+                mean_out[slot, start : start + half, :] = rows * (1.0 / SCALE_IN)
         return carry
 
-    lax.fori_loop(0, blocks, read_mean, 0)
-
-    def shift_back(tile, kind, v):
-        return tile if OFFSETS[kind][v] == 0.0 else tile + OFFSETS[kind][v]
+    lax.fori_loop(0, blocks, read_mean, 0, unroll=4)
 
     def core(kind, slot, v):
-        return shift_back(arrived[kind * blocks + slot, tile_rows(plan, v), :], kind, v)
+        return arrived[kind * blocks + slot, tile_rows(plan, v), :]
 
     def x_halo(kind, slot, v, end):
         at = plan.x_base + end * count + v
-        return shift_back(arrived[kind * blocks + slot, at : at + 1, :], kind, v)
+        return arrived[kind * blocks + slot, pl.ds(at, xs, stride=0), :]
 
     def y_halo(kind, slot, v, end):
         base = plan.y_base + (v // 2) * xs
         tile = arrived[kind * blocks + slot, base : base + xs, :]
-        if v % 2 == 1:
-            tile = roll_lanes(tile, LANES // 2)
-        return shift_back(tile, kind, v)
+        return roll_lanes(tile, LANES // 2) if v % 2 == 1 else tile
 
     def mean(slot):
         return [mean_out[slot, tile_rows(plan, v), :] for v in range(count)]
 
-    def store(kind, slot, tiles):
-        m = kind * blocks + slot
-        quarter = m % 4
-        rest = plan.devices * xs + (m // 4) * xs
-        up = down = None
-        for v, tile in enumerate(tiles):
-            after[m, tile_rows(plan, v), :] = tile
-            coded = (tile - OFFSETS[kind][v]) * SCALE_MID
-            x_up_raw[pl.ds(m * count + v, 1), :] = coded[xs - 1 : xs]
-            x_down_raw[pl.ds(m * count + v, 1), :] = coded[0:1]
-            if v < 4:
-                high = roll_lanes(coded, side * (v + 1))
-                low = roll_lanes(coded, side * v)
-                mine = lane >= side * v
-                up = high if v == 0 else jnp.where(mine, high, up)
-                down = low if v == 0 else jnp.where(mine, low, down)
-            else:
-                high = pltpu.roll(coded, (side * (quarter + 1)) % LANES, 1)
-                low = pltpu.roll(coded, side * quarter, 1)
-                mine = lane >= side * quarter
-                where = pl.ds(pl.multiple_of(rest, xs), xs)
-                y_up_raw[where, :] = jnp.where(mine, high, y_up_raw[where, :])
-                y_down_raw[where, :] = jnp.where(mine, low, y_down_raw[where, :])
-        where = pl.ds(pl.multiple_of(m * xs, xs), xs)
-        y_up_raw[where, :] = up
-        y_down_raw[where, :] = down
-
-    advance(plan, table, core, x_halo, y_halo, mean, lamb, store)
+    def in_quarters(tiles, first):
+        packed = None
+        for quarter, tile in enumerate(tiles):
+            moved = roll_lanes(tile, side * (quarter - first))
+            packed = moved if packed is None else jnp.where(lane >= side * quarter, moved, packed)
+        return packed
+
+    def store(kind, quad, results):
+        rest = []
+        for r, tiles in enumerate(results):
+            m = kind * blocks + quad * 4 + r
+            coded = []
+            for v, tile in enumerate(tiles):
+                after[m, tile_rows(plan, v), :] = tile
+                offset = OFFSETS[kind][v] * SCALE_MID
+                coded.append(tile if offset == 0.0 else tile - offset)
+                x_up_raw[pl.ds(m * count + v, 1), :] = coded[v][xs - 1 : xs]
+                x_down_raw[pl.ds(m * count + v, 1), :] = coded[v][0:1]
+            rest.append(coded[4])
+            where = pl.ds(pl.multiple_of(m * xs, xs), xs)
+            y_up_raw[where, :] = in_quarters(coded[:4], 3)
+            y_down_raw[where, :] = in_quarters(coded[:4], 0)
+        start = (plan.devices + kind * (blocks // 4) + quad) * xs
+        where = pl.ds(pl.multiple_of(start, xs), xs)
+        y_up_raw[where, :] = in_quarters(rest, 3)
+        y_down_raw[where, :] = in_quarters(rest, 0)
+
+    def les_part(slot):
+        return les_z(plan, table, slot, core, SCALE_IN)
+
+    def ac_part(slot):
+        return ac_z(plan, table, slot, core, mean)
+
+    advance(plan, table, core, x_halo, y_halo, mean, lamb, les_part, ac_part, store)
     for raw, out in (
         (x_up_raw, x_up), (x_down_raw, x_down), (y_up_raw, y_up), (y_down_raw, y_down),
     ):
         out[...] = to_wire(raw[...])
 
 
+def middle_kernel(plan, table, before, mean_in, les_out, ac_out):
+    def core(kind, slot, v):
+        return before[kind * plan.blocks + slot, tile_rows(plan, v), :]
+
+    def mean(slot):
+        return [mean_in[slot, tile_rows(plan, v), :] for v in range(plan.vars)]
+
+    def body(slot, carry):
+        for i, tile in enumerate(les_z(plan, table, slot, core, SCALE_MID)):
+            les_out[slot, tile_rows(plan, i), :] = tile
+        for v, tile in enumerate(ac_z(plan, table, slot, core, mean)):
+            ac_out[slot, tile_rows(plan, v), :] = tile
+        return carry
+
+    lax.fori_loop(0, plan.blocks, body, 0, unroll=2)
+
+
 def last_kernel(
-    plan, table, before, mean_in, x_low, x_high, y_low, y_high,
+    plan, table, before, mean_in, les_in, ac_in, x_low, x_high, y_low, y_high,
     message, lamb, x_low_raw, x_high_raw, y_low_raw, y_high_raw, coded,
 ):
     xs, side, count, blocks = plan.xs, plan.side, plan.vars, plan.blocks
     for raw, sent in (
         (x_low_raw, x_low), (x_high_raw, x_high), (y_low_raw, y_low), (y_high_raw, y_high),
     ):
-        raw[...] = from_wire(sent[...]) * (1.0 / SCALE_MID)
+        raw[...] = from_wire(sent[...])
 
     def shift_back(tile, kind, v):
-        return tile if OFFSETS[kind][v] == 0.0 else tile + OFFSETS[kind][v]
+        offset = OFFSETS[kind][v] * SCALE_MID
+        return tile if offset == 0.0 else tile + offset
 
     def core(kind, slot, v):
         return before[kind * blocks + slot, tile_rows(plan, v), :]
@@ -417,7 +493,7 @@
     def x_halo(kind, slot, v, end):
         raw = x_high_raw if end else x_low_raw
         at = (kind * blocks + slot) * count + v
-        return shift_back(raw[pl.ds(at, 1), :], kind, v)
+        return shift_back(raw[pl.ds(at, xs, stride=0), :], kind, v)
 
     def y_halo(kind, slot, v, end):
         raw = y_high_raw if end else y_low_raw
@@ -427,25 +503,34 @@
             tile = raw[pl.ds(pl.multiple_of(m * xs, xs), xs), :]
             tile = roll_lanes(tile, target - side * v)
         else:
-            rest = plan.devices * xs + (m // 4) * xs
+            rest = plan.devices * xs + (m >> 2) * xs
             tile = raw[pl.ds(pl.multiple_of(rest, xs), xs), :]
-            tile = pltpu.roll(tile, (target + LANES - side * (m % 4)) % LANES, 1)
+            tile = pltpu.roll(tile, (target + LANES - side * (m & 3)) & (LANES - 1), 1)
         return shift_back(tile, kind, v)
 
     def mean(slot):
         return [mean_in[slot, tile_rows(plan, v), :] for v in range(count)]
 
-    def store(kind, slot, tiles):
-        for v, tile in enumerate(tiles):
-            coded[kind * blocks + slot, tile_rows(plan, v), :] = (tile - OFFSETS[kind][v]) * SCALE_OUT
-
-    advance(plan, table, core, x_halo, y_halo, mean, lamb, store)
+    def store(kind, quad, results):
+        for r, tiles in enumerate(results):
+            for v, tile in enumerate(tiles):
+                offset = OFFSETS[kind][v] * SCALE_OUT
+                tile = tile if offset == 0.0 else tile - offset
+                coded[kind * blocks + quad * 4 + r, tile_rows(plan, v), :] = tile
+
+    def les_part(slot):
+        return [les_in[slot, tile_rows(plan, i), :] for i in range(count + 5)]
+
+    def ac_part(slot):
+        return [ac_in[slot, tile_rows(plan, v), :] for v in range(count)]
+
+    advance(plan, table, core, x_halo, y_halo, mean, lamb, les_part, ac_part, store)
 
     def write(m, carry):
         message[m] = to_wire(coded[m])
         return carry
 
-    lax.fori_loop(0, plan.devices, write, 0, unroll=2)
+    lax.fori_loop(0, plan.devices, write, 0, unroll=4)
 
 
 def unpack_kernel(plan, message, out):
@@ -487,7 +572,7 @@
         functools.partial(pack_kernel, plan),
         out_shape=(
             array(WIRE, devices, plan.rows, LANES),
-            array(jnp.int32, 2 * COLUMNS * blocks),
+            pltpu.SMEM((2 * COLUMNS * blocks,), jnp.int32),
         ),
         in_specs=[pl.BlockSpec(memory_space=pltpu.HBM)] * len(far),
         out_specs=tuple(vmem(1) + smem(1)),
@@ -514,24 +599,40 @@
         ),
         in_specs=smem(1) + vmem(1),
         out_specs=tuple(vmem(6)),
-        scratch_shapes=[pltpu.VMEM((devices, plan.rows, LANES), f32), lamb_scratch] + halo_scratch,
+        scratch_shapes=[
+            pltpu.VMEM((devices, plan.rows, LANES), f32),
+            pltpu.VMEM((2, plan.rows, LANES), f32),
+            lamb_scratch,
+        ]
+        + halo_scratch,
         name="first_step",
         compiler_params=pltpu.CompilerParams(vmem_limit_bytes=16 * 1024 * 1024),
     )(table, message)
     moves = [plan.permutation(*step) for step in ((1, 0), (-1, 0), (0, 1), (0, -1))]
     halos = [lax.ppermute(halo, axes, move) for halo, move in zip(halos, moves)]
 
+    parts = pl.pallas_call(
+        functools.partial(middle_kernel, plan),
+        out_shape=(
+            array(f32, blocks, (count + 5) * xs, LANES),
+            array(f32, blocks, plan.core_rows, LANES),
+        ),
+        in_specs=smem(1) + vmem(2),
+        out_specs=tuple(vmem(2)),
+        name="middle",
+        compiler_params=pltpu.CompilerParams(vmem_limit_bytes=16 * 1024 * 1024),
+    )(table, after, mean)
     message = pl.pallas_call(
         functools.partial(last_kernel, plan),
         out_shape=array(WIRE, devices, plan.core_rows, LANES),
-        in_specs=smem(1) + vmem(6),
+        in_specs=smem(1) + vmem(8),
         out_specs=vmem(1)[0],
         scratch_shapes=[lamb_scratch]
         + halo_scratch
         + [pltpu.VMEM((devices, plan.core_rows, LANES), f32)],
         name="last_step",
         compiler_params=pltpu.CompilerParams(vmem_limit_bytes=16 * 1024 * 1024),
-    )(table, after, mean, *halos)
+    )(table, after, mean, *parts, *halos)
     message = lax.all_to_all(message, axes, split_axis=0, concat_axis=0, tiled=True)
 
     result = pl.pallas_call(

time: 60.4 us -> 58.4 us (0.967)
  Pallas kernels: 9.45 us -> 8.38 us
  waiting for transfers between devices: 1.98 us -> 1.05 us
    pallas_call x1, Pallas kernels: 2.86 us -> 1.79 us  [on_device(): pl.pallas_call(functools.partial(last_kernel, plan), out_shape=array(WIRE...]
    ppermute x4, waiting for transfers between devices: 1.98 us -> 1.05 us  [on_device(): halos = [lax.ppermute(halo, axes, move) for halo, move in zip(halos, moves)]]
    pallas_call x0 -> x1, Pallas kernels: none -> 0.92 us  [on_device(): pl.pallas_call(functools.partial(middle_kernel, plan), out_shape=(array(f...]
    pallas_call x1, Pallas kernels: 3.32 us -> 2.71 us  [on_device(): pl.pallas_call(functools.partial(first_kernel, plan), out_shape=(array(f3...]
  transfers between devices with their start and end apart: 4 -> 4, of which waited for: 1 -> 1; matrix products, arithmetic and copies ran while one was open for 0% -> 0% of each run, Pallas kernels for 0% -> 2%
where the time goes in v3:
time: 58.4 us; the launch traced here: 58.2 us
  blocking collectives  44.6 us (76%)
  Pallas kernels  8.38 us (14%)
  starting transfers between devices  4.1 us (7%)
  waiting for transfers between devices  1.05 us (2%)
    all_to_all x2, blocking collectives, on_device(): lax.all_to_all(message, axes, split_axis=0, concat_axis=0, tiled=True)  44.6 us
    ppermute x4, starting transfers between devices, on_device(): halos = [lax.ppermute(halo, axes, move) for halo, move in zip(halos, moves)]  4.1 us
    pallas_call x1, Pallas kernels, on_device(): pl.pallas_call(functools.partial(first_kernel, plan), out_shape=(array(f3...  2.71 us
    pallas_call x1, Pallas kernels, on_device(): pl.pallas_call(functools.partial(pack_kernel, plan), out_shape=(array(WIR...  2.04 us
    pallas_call x1, Pallas kernels, on_device(): pl.pallas_call(functools.partial(last_kernel, plan), out_shape=array(WIRE...  1.79 us
  transfers between devices with their start and end apart: 4, of which 1 were waited for; matrix products, arithmetic and copies ran while one was open for 0% of the time, Pallas kernels for 2%

profile of v3, /device:TPU:0, one launch (start us, length us, event | category | flops | bytes accessed | tf_op | source)
XLA Modules:
  0.0 58.2 jit_solution(16554363696785963605)
XLA Ops:
  0.0 2.0 %pack.1 = (s16[32,96,128]{2,1,0:T(8,128)(2,1)S(1)}, s32[224]{0:T(256)S(4)}) custom-call(f32[5,32,1024]{2,1,0:T(8,128)} %bitcast.5, f32[5,32,1024]{2,1,0:T(8,128)} %bitcast.6, s32[16]{0:T(128)} %refs_0_.1, s32[16]{0:T(128)} %refs_1_.1, s32[6,16]{1,0:T(8,128)} %bitcast.7, s32[6,16]{1,0:T(8,128)} %bitcast.8, s32[16]{0:T(128)} %refs_4_.1), custom_call_target="tpu_custom_call" | custom-call | tf_op jit(solution)/shard_map/pack/pallas_call | solution.py:571
  2.0 29.6 %all_to_all.10.message = s16[32,96,128]{2,1,0:T(8,128)(2,1)S(1)} all-to-all(s16[32,96,128]{2,1,0:T(8,128)(2,1)S(1)} %get-tuple-element.16), channel_id=1, replica_groups=mesh['section'=2,'block'=16] {'section','block'}, dimensions={0} | all-to-all | bytes 1572864 | tf_op jit(solution)/shard_map/all_to_all | solution.py:586
  31.6 2.7 %first_step.1 = (f32[32,40,128]{2,1,0:T(8,128)S(1)}, f32[16,40,128]{2,1,0:T(8,128)S(1)}, s16[160,128]{1,0:T(8,128)(2,1)S(1)}, s16[160,128]{1,0:T(8,128)(2,1)S(1)...) custom-call(s32[224]{0:T(256)S(4)} %get-tuple-element.15.table, s16[32,96,128]{2,1,0:T(8,128)(2,1)S(1)} %all_to_all.10.message), custom_call_target="tpu_custom_call" | custom-call | tf_op jit(solution)/shard_map/first_step/pallas_call | solution.py:593
  34.3 0.1 collective-permute-start.2
  34.4 2.0 %collective-permute-start.3 = (s16[320,128]{1,0:T(8,128)(2,1)S(1)}, s16[320,128]{1,0:T(8,128)(2,1)S(1)}, u32[]{:S(2)}, u32[]{:S(2)}) collective-permute-start(s16[320,128]{1,0:T(8,128)(2,1)S(1)} %get-tuple-element.24), channel_id=1, source_target_pairs={{0,2},{1,3},{2,6},{3,7},{4,0},{5,1},{6,10},{7,11},{8,4},{9,5},{10,... | collective-permute-start | bytes 245768 | tf_op jit(solution)/shard_map/ppermute | solution.py:612
  36.4 0.0 collective-permute-start
  36.4 2.0 %collective-permute-start.1 = (s16[160,128]{1,0:T(8,128)(2,1)S(1)}, s16[160,128]{1,0:T(8,128)(2,1)S(1)}, u32[]{:S(2)}, u32[]{:S(2)}) collective-permute-start(s16[160,128]{1,0:T(8,128)(2,1)S(1)} %get-tuple-element.22), channel_id=1, source_target_pairs={{0,1},{1,17},{2,3},{3,19},{4,5},{5,21},{6,7},{7,23},{8,9},{9,25},{... | collective-permute-start | bytes 122888 | tf_op jit(solution)/shard_map/ppermute | solution.py:612
  38.4 0.9 %middle.1 = (f32[16,80,128]{2,1,0:T(8,128)S(1)}, f32[16,40,128]{2,1,0:T(8,128)S(1)}) custom-call(s32[224]{0:T(256)S(4)} %get-tuple-element.15.table, f32[32,40,128]{2,1,0:T(8,128)S(1)} %get-tuple-element.17.before, f32[16,40,128]{2,1,0:T(8,128)S(1)} %get-tuple-element.18.mean_in), custom_call_target="tpu_custom_call" | custom-call | tf_op jit(solution)/shard_map/middle/pallas_call | solution.py:614
  39.4 1.0 %collective-permute-done.x_low = s16[160,128]{1,0:T(8,128)(2,1)S(1)} collective-permute-done((s16[160,128]{1,0:T(8,128)(2,1)S(1)}, s16[160,128]{1,0:T(8,128)(2,1)S(1)}, u32[]{:S(2)}, u32[]{:S(2)}) %collective-permute-start) | collective-permute-done | bytes 40992 | tf_op jit(solution)/shard_map/ppermute | solution.py:612
  40.4 0.0 collective-permute-done.1.x_high
  40.4 0.0 collective-permute-done.2.y_low
  40.4 0.0 collective-permute-done.3.y_high
  40.4 1.8 %last_step.1 = s16[32,40,128]{2,1,0:T(8,128)(2,1)S(1)} custom-call(s32[224]{0:T(256)S(4)} %get-tuple-element.15.table, f32[32,40,128]{2,1,0:T(8,128)S(1)} %get-tuple-element.17.before, f32[16,40,128]{2,1,0:T(8,128)S(1)} %get-tuple-element.18.mean_in, f32[16,80,128]{2,1,0:T(8,128)S(1)} %get-tuple-element.19.les_in, ...), custom_call_target="tpu_custom_call" | custom-call | tf_op jit(solution)/shard_map/last_step/pallas_call | solution.py:625
  42.2 15.1 %all_to_all.11.message = s16[32,40,128]{2,1,0:T(8,128)(2,1)S(1)} all-to-all(s16[32,40,128]{2,1,0:T(8,128)(2,1)S(1)} %last_step.1), channel_id=1, replica_groups=mesh['section'=2,'block'=16] {'section','block'}, dimensions={0} | all-to-all | bytes 655360 | tf_op jit(solution)/shard_map/all_to_all | solution.py:636
  57.3 0.9 %unpack.1 = f32[5,32,1024]{2,1,0:T(8,128)} custom-call(s16[32,40,128]{2,1,0:T(8,128)(2,1)S(1)} %all_to_all.11.message), custom_call_target="tpu_custom_call" | custom-call | tf_op jit(solution)/shard_map/unpack/pallas_call | solution.py:638
Async XLA Ops:
  34.3 6.1 %collective-permute-start.2 = (s16[320,128]{1,0:T(8,128)(2,1)S(1)}, s16[320,128]{1,0:T(8,128)(2,1)S(1)}, u32[]{:S(2)}, u32[]{:S(2)}) collective-permute-start(s16[320,128]{1,0:T(8,128)(2,1)S(1)} %get-tuple-element.23), channel_id=1, source_target_pairs={{0,4},{1,5},{2,0},{3,1},{4,8},{5,9},{6,2},{7,3},{8,12},{9,13},{10,... | collective-permute-start | bytes 245768 | tf_op jit(solution)/shard_map/ppermute | solution.py:612
  34.4 6.0 %collective-permute-start.3 = (s16[320,128]{1,0:T(8,128)(2,1)S(1)}, s16[320,128]{1,0:T(8,128)(2,1)S(1)}, u32[]{:S(2)}, u32[]{:S(2)}) collective-permute-start(s16[320,128]{1,0:T(8,128)(2,1)S(1)} %get-tuple-element.24), channel_id=1, source_target_pairs={{0,2},{1,3},{2,6},{3,7},{4,0},{5,1},{6,10},{7,11},{8,4},{9,5},{10,... | collective-permute-start | bytes 245768 | tf_op jit(solution)/shard_map/ppermute | solution.py:612
  36.4 4.0 %collective-permute-start = (s16[160,128]{1,0:T(8,128)(2,1)S(1)}, s16[160,128]{1,0:T(8,128)(2,1)S(1)}, u32[]{:S(2)}, u32[]{:S(2)}) collective-permute-start(s16[160,128]{1,0:T(8,128)(2,1)S(1)} %get-tuple-element.21), channel_id=1, source_target_pairs={{0,16},{1,0},{2,18},{3,2},{4,20},{5,4},{6,22},{7,6},{8,24},{9,8},{... | collective-permute-start | bytes 122888 | tf_op jit(solution)/shard_map/ppermute | solution.py:612
  36.4 4.0 %collective-permute-start.1 = (s16[160,128]{1,0:T(8,128)(2,1)S(1)}, s16[160,128]{1,0:T(8,128)(2,1)S(1)}, u32[]{:S(2)}, u32[]{:S(2)}) collective-permute-start(s16[160,128]{1,0:T(8,128)(2,1)S(1)} %get-tuple-element.22), channel_id=1, source_target_pairs={{0,1},{1,17},{2,3},{3,19},{4,5},{5,21},{6,7},{7,23},{8,9},{9,25},{... | collective-permute-start | bytes 122888 | tf_op jit(solution)/shard_map/ppermute | solution.py:612

commit v4 on v3

--- a/solution.py
+++ b/solution.py
@@ -45,7 +45,7 @@
         self.mean_base = self.y_base + len(PAIRS) * self.xs
         self.x_base = self.mean_base + num_vars * self.half
         self.rows = -(-(self.x_base + 2 * num_vars) // 16) * 16
-        assert sections == 2 and LANES == 4 * side and 2 * self.half * self.nx == side
+        assert self.nx > 1 and sections == 2 and LANES == 4 * side and 2 * self.half * self.nx == side
 
     def piece(self, device):
         section, block = device // self.blocks, device % self.blocks
@@ -100,8 +100,8 @@
 ):
     lookups_hbm, (message, table), rest = refs[:5], refs[5:7], refs[7:]
     lookups, rest = rest[:5], rest[5:]
-    state, mean, filled, les_inv, ac_inv, pair_inv, small_sem, state_sem, mean_sem = rest
-    les_owner, ac_owner, les_nbr, ac_nbr, coupling = lookups
+    state, mean, filled, *found = rest[:-3]
+    small_sem, state_sem, mean_sem = rest[-3:]
     small = [
         pltpu.make_async_copy(source, target, small_sem.at[i])
         for i, (source, target) in enumerate(zip(lookups_hbm, lookups))
@@ -118,76 +118,101 @@
     px, py = plan.own_piece(section, lax.axis_index("block"))
     for copy in small:
         copy.wait()
-    look_up(plan, px, py, table, lookups, les_inv, ac_inv, pair_inv)
-    for copy in large:
-        copy.wait()
+    invert(plan, lookups, *found)
 
     xs, side, half = plan.xs, plan.side, plan.half
     width = side * side
-    offsets = [jnp.where(section == 0, OFFSETS[0][v], OFFSETS[1][v]) for v in range(plan.vars)]
-    for v in range(plan.vars):
-        state[v] = (state[v] - offsets[v]) * SCALE_IN
     lane = lane_index(xs)
+    outer = (lane < side) | (lane >= LANES - side)
+    pieces = []
     for device in range(plan.devices):
         tx, ty = plan.piece(device)
-        x0, l0 = tx * xs, ty * LANES
-        here = slice(l0, l0 + LANES)
-        before = (l0 - LANES) % width
-        after = (l0 + LANES) % width
-        for v in range(plan.vars):
-            filled[device, v * xs : (v + 1) * xs, :] = state[v, x0 : x0 + xs, here]
+        pieces.append((device, tx * xs, ty * LANES))
+    whole = xs % 8 == 0
+    gathered = plan.mean_base if whole else 0
+
+    def put(device, start, tile):
+        if whole:
+            message[device, start : start + xs, :] = to_wire(tile)
+        else:
+            filled[device, start : start + xs, :] = tile
+
+    used = plan.x_base + 2 * plan.vars
+    for v in range(plan.vars):
+        large[2 * v].wait()
+        for slot in range(v * plan.blocks // plan.vars, (v + 1) * plan.blocks // plan.vars):
+            look_up(plan, px, py, table, lookups, *found, slot)
+        offset = jnp.where(section == 0, OFFSETS[0][v], OFFSETS[1][v])
+        state[v] = (state[v] - offset) * SCALE_IN
+        for device, x0, l0 in pieces:
+            here = slice(l0, l0 + LANES)
+            put(device, v * xs, state[v, x0 : x0 + xs, here])
             filled[device, plan.x_base + v, :] = state[v, (x0 - 1) % side, here]
             filled[device, plan.x_base + plan.vars + v, :] = state[v, (x0 + xs) % side, here]
+        if v % 2 == 1 or v == plan.vars - 1:
+            i, (a, b) = v // 2, PAIRS[v // 2]
+            for device, x0, l0 in pieces:
+                before = (l0 - LANES) % width
+                after = (l0 + LANES) % width
+                edge = [
+                    jnp.where(
+                        lane >= LANES - side,
+                        state[u, x0 : x0 + xs, before : before + LANES],
+                        state[u, x0 : x0 + xs, after : after + LANES],
+                    )
+                    for u in ((a, b) if a != b else (a,))
+                ]
+                tile = edge[0]
+                if a != b:
+                    tile = jnp.where(outer, edge[0], roll_lanes(edge[1], LANES // 2))
+                put(device, plan.y_base + i * xs, tile)
+        large[2 * v + 1].wait()
+        for device, x0, l0 in pieces:
+            here = slice(l0, l0 + LANES)
             first, second = mean[v, x0 : x0 + half, here], mean[v, x0 + half : x0 + xs, here]
             piece = jnp.where(section == 0, first, second)
             base = plan.mean_base + v * half
             filled[device, base : base + half, :] = (piece - MEAN_OFFSETS[v]) * SCALE_IN
-        for i, (a, b) in enumerate(PAIRS):
-            edge = [
-                jnp.where(
-                    lane >= LANES - side,
-                    state[v, x0 : x0 + xs, before : before + LANES],
-                    state[v, x0 : x0 + xs, after : after + LANES],
-                )
-                for v in ((a, b) if a != b else (a,))
-            ]
-            tile = edge[0]
-            if a != b:
-                outer = (lane < side) | (lane >= LANES - side)
-                tile = jnp.where(outer, edge[0], roll_lanes(edge[1], LANES // 2))
-            base = plan.y_base + i * xs
-            filled[device, base : base + xs, :] = tile
-        used = plan.x_base + 2 * plan.vars
+    for device, _, _ in pieces:
         if used < plan.rows:
             filled[device, used:, :] = jnp.zeros((plan.rows - used, LANES), jnp.float32)
-        message[device] = to_wire(filled[device])
-
-
-def look_up(plan, px, py, table, lookups, les_inv, ac_inv, pair_inv):
+        message[device, gathered:, :] = to_wire(filled[device, gathered:, :])
+
+
+def invert(plan, lookups, les_inv, ac_inv, pair_inv, les_slots, ac_slots):
+    les_owner, ac_owner, _, _, coupling = lookups
+    les_slots[0] = -1
+    ac_slots[0] = -1
+    for i in range(plan.blocks):
+        les, ac = les_owner[i], ac_owner[i]
+        les_inv[les] = i
+        ac_inv[ac] = i
+        les_slots[i + 1] = les
+        ac_slots[i + 1] = ac
+        pair_inv[coupling[i]] = i
+
+
+def look_up(plan, px, py, table, lookups, les_inv, ac_inv, pair_inv, les_slots, ac_slots, slot):
     les_owner, ac_owner, les_nbr, ac_nbr, coupling = lookups
-    for i in range(plan.blocks):
-        les_inv[les_owner[i]] = i
-        ac_inv[ac_owner[i]] = i
-        pair_inv[coupling[i]] = i
-    at_edge = (px == 0, px == plan.nx - 1, py == 0, py == plan.ny - 1, True, True)
-    faces = FACES if plan.layers_z > 1 else 4
-    for slot in range(plan.blocks):
-        les_block = les_inv[slot]
-        ac_block = ac_inv[slot]
-        for kind, (block, nbr, owner) in enumerate(
-            ((les_block, les_nbr, les_owner), (ac_block, ac_nbr, ac_owner))
-        ):
-            for face in range(FACES):
-                if face < faces:
-                    other = nbr[face, block]
-                    source = jnp.where(other < 0, -1, owner[jnp.maximum(other, 0)])
-                    if face < 4:
-                        source = jnp.where(at_edge[face], source, slot)
-                else:
-                    source = -1
-                table[(kind * COLUMNS + face) * plan.blocks + slot] = source
-        table[FACES * plan.blocks + slot] = ac_owner[pair_inv[les_block]]
-        table[(COLUMNS + FACES) * plan.blocks + slot] = les_owner[coupling[ac_block]]
+    les_block = les_inv[slot]
+    ac_block = ac_inv[slot]
+    for kind, (block, nbr, slots) in enumerate(
+        ((les_block, les_nbr, les_slots), (ac_block, ac_nbr, ac_slots))
+    ):
+
+        def write(face, value):
+            table[(kind * COLUMNS + face) * plan.blocks + slot] = value
+
+        for axis, (at, count) in enumerate(((px, plan.nx), (py, plan.ny))):
+            low, high = at == 0, at == count - 1
+            source = slots[nbr[jnp.where(low, 2 * axis, 2 * axis + 1), block] + 1]
+            write(2 * axis, jnp.where(low, source, slot))
+            write(2 * axis + 1, jnp.where(high, source, slot))
+        if plan.layers_z > 1:
+            for face in (4, 5):
+                write(face, slots[nbr[face, block] + 1])
+    table[FACES * plan.blocks + slot] = ac_owner[pair_inv[les_block]]
+    table[(COLUMNS + FACES) * plan.blocks + slot] = les_owner[coupling[ac_block]]
 
 
 def sides_xy(plan, table, kind, slot, own, x_halo, y_halo):
@@ -579,6 +604,7 @@
         scratch_shapes=lookups
         + [volume, volume, pltpu.VMEM((devices, plan.rows, LANES), f32)]
         + [pltpu.SMEM((blocks,), jnp.int32)] * 3
+        + [pltpu.SMEM((blocks + 1,), jnp.int32)] * 2
         + [pltpu.SemaphoreType.DMA((n,)) for n in (len(lookups), count, count)],
         name="pack",
         compiler_params=pltpu.CompilerParams(vmem_limit_bytes=16 * 1024 * 1024),

time: 58.4 us -> 58.2 us (level)
  no operation moved by 1% of the time
where the time goes in v4:
time: 58.2 us; the launch traced here: 58 us
  blocking collectives  44.6 us (77%)
  Pallas kernels  8.2 us (14%)
  starting transfers between devices  4.1 us (7%)
  waiting for transfers between devices  1.05 us (2%)
    all_to_all x2, blocking collectives, on_device(): lax.all_to_all(message, axes, split_axis=0, concat_axis=0, tiled=True)  44.6 us
    ppermute x4, starting transfers between devices, on_device(): halos = [lax.ppermute(halo, axes, move) for halo, move in zip(halos, moves)]  4.1 us
    pallas_call x1, Pallas kernels, on_device(): pl.pallas_call(functools.partial(first_kernel, plan), out_shape=(array(f3...  2.71 us
    pallas_call x1, Pallas kernels, on_device(): pl.pallas_call(functools.partial(pack_kernel, plan), out_shape=(array(WIR...  1.86 us
    pallas_call x1, Pallas kernels, on_device(): pl.pallas_call(functools.partial(last_kernel, plan), out_shape=array(WIRE...  1.79 us
  transfers between devices with their start and end apart: 4, of which 1 were waited for; matrix products, arithmetic and copies ran while one was open for 0% of the time, Pallas kernels for 2%

profile of v4, /device:TPU:0, one launch (start us, length us, event | category | flops | bytes accessed | tf_op | source)
XLA Modules:
  0.0 58.0 jit_solution(16729148425864633998)
XLA Ops:
  0.0 1.9 %pack.1 = (s16[32,96,128]{2,1,0:T(8,128)(2,1)S(1)}, s32[224]{0:T(256)S(4)}) custom-call(f32[5,32,1024]{2,1,0:T(8,128)} %bitcast.5, f32[5,32,1024]{2,1,0:T(8,128)} %bitcast.6, s32[16]{0:T(128)} %refs_0_.1, s32[16]{0:T(128)} %refs_1_.1, s32[6,16]{1,0:T(8,128)} %bitcast.7, s32[6,16]{1,0:T(8,128)} %bitcast.8, s32[16]{0:T(128)} %refs_4_.1), custom_call_target="tpu_custom_call" | custom-call | tf_op jit(solution)/shard_map/pack/pallas_call | solution.py:596
  1.9 29.6 %all_to_all.10.message = s16[32,96,128]{2,1,0:T(8,128)(2,1)S(1)} all-to-all(s16[32,96,128]{2,1,0:T(8,128)(2,1)S(1)} %get-tuple-element.16), channel_id=1, replica_groups=mesh['section'=2,'block'=16] {'section','block'}, dimensions={0} | all-to-all | bytes 1572864 | tf_op jit(solution)/shard_map/all_to_all | solution.py:612
  31.4 2.7 %first_step.1 = (f32[32,40,128]{2,1,0:T(8,128)S(1)}, f32[16,40,128]{2,1,0:T(8,128)S(1)}, s16[160,128]{1,0:T(8,128)(2,1)S(1)}, s16[160,128]{1,0:T(8,128)(2,1)S(1)...) custom-call(s32[224]{0:T(256)S(4)} %get-tuple-element.15.table, s16[32,96,128]{2,1,0:T(8,128)(2,1)S(1)} %all_to_all.10.message), custom_call_target="tpu_custom_call" | custom-call | tf_op jit(solution)/shard_map/first_step/pallas_call | solution.py:619
  34.1 0.1 collective-permute-start.2
  34.2 2.0 %collective-permute-start.3 = (s16[320,128]{1,0:T(8,128)(2,1)S(1)}, s16[320,128]{1,0:T(8,128)(2,1)S(1)}, u32[]{:S(2)}, u32[]{:S(2)}) collective-permute-start(s16[320,128]{1,0:T(8,128)(2,1)S(1)} %get-tuple-element.24), channel_id=1, source_target_pairs={{0,2},{1,3},{2,6},{3,7},{4,0},{5,1},{6,10},{7,11},{8,4},{9,5},{10,... | collective-permute-start | bytes 245768 | tf_op jit(solution)/shard_map/ppermute | solution.py:638
  36.2 0.0 collective-permute-start
  36.2 2.0 %collective-permute-start.1 = (s16[160,128]{1,0:T(8,128)(2,1)S(1)}, s16[160,128]{1,0:T(8,128)(2,1)S(1)}, u32[]{:S(2)}, u32[]{:S(2)}) collective-permute-start(s16[160,128]{1,0:T(8,128)(2,1)S(1)} %get-tuple-element.22), channel_id=1, source_target_pairs={{0,1},{1,17},{2,3},{3,19},{4,5},{5,21},{6,7},{7,23},{8,9},{9,25},{... | collective-permute-start | bytes 122888 | tf_op jit(solution)/shard_map/ppermute | solution.py:638
  38.2 0.9 %middle.1 = (f32[16,80,128]{2,1,0:T(8,128)S(1)}, f32[16,40,128]{2,1,0:T(8,128)S(1)}) custom-call(s32[224]{0:T(256)S(4)} %get-tuple-element.15.table, f32[32,40,128]{2,1,0:T(8,128)S(1)} %get-tuple-element.17.before, f32[16,40,128]{2,1,0:T(8,128)S(1)} %get-tuple-element.18.mean_in), custom_call_target="tpu_custom_call" | custom-call | tf_op jit(solution)/shard_map/middle/pallas_call | solution.py:640
  39.2 1.0 %collective-permute-done.x_low = s16[160,128]{1,0:T(8,128)(2,1)S(1)} collective-permute-done((s16[160,128]{1,0:T(8,128)(2,1)S(1)}, s16[160,128]{1,0:T(8,128)(2,1)S(1)}, u32[]{:S(2)}, u32[]{:S(2)}) %collective-permute-start) | collective-permute-done | bytes 40992 | tf_op jit(solution)/shard_map/ppermute | solution.py:638
  40.2 0.0 collective-permute-done.1.x_high
  40.2 0.0 collective-permute-done.2.y_low
  40.2 0.0 collective-permute-done.3.y_high
  40.2 1.8 %last_step.1 = s16[32,40,128]{2,1,0:T(8,128)(2,1)S(1)} custom-call(s32[224]{0:T(256)S(4)} %get-tuple-element.15.table, f32[32,40,128]{2,1,0:T(8,128)S(1)} %get-tuple-element.17.before, f32[16,40,128]{2,1,0:T(8,128)S(1)} %get-tuple-element.18.mean_in, f32[16,80,128]{2,1,0:T(8,128)S(1)} %get-tuple-element.19.les_in, ...), custom_call_target="tpu_custom_call" | custom-call | tf_op jit(solution)/shard_map/last_step/pallas_call | solution.py:651
  42.0 15.1 %all_to_all.11.message = s16[32,40,128]{2,1,0:T(8,128)(2,1)S(1)} all-to-all(s16[32,40,128]{2,1,0:T(8,128)(2,1)S(1)} %last_step.1), channel_id=1, replica_groups=mesh['section'=2,'block'=16] {'section','block'}, dimensions={0} | all-to-all | bytes 655360 | tf_op jit(solution)/shard_map/all_to_all | solution.py:662
  57.1 0.9 %unpack.1 = f32[5,32,1024]{2,1,0:T(8,128)} custom-call(s16[32,40,128]{2,1,0:T(8,128)(2,1)S(1)} %all_to_all.11.message), custom_call_target="tpu_custom_call" | custom-call | tf_op jit(solution)/shard_map/unpack/pallas_call | solution.py:664
Async XLA Ops:
  34.1 6.1 %collective-permute-start.2 = (s16[320,128]{1,0:T(8,128)(2,1)S(1)}, s16[320,128]{1,0:T(8,128)(2,1)S(1)}, u32[]{:S(2)}, u32[]{:S(2)}) collective-permute-start(s16[320,128]{1,0:T(8,128)(2,1)S(1)} %get-tuple-element.23), channel_id=1, source_target_pairs={{0,4},{1,5},{2,0},{3,1},{4,8},{5,9},{6,2},{7,3},{8,12},{9,13},{10,... | collective-permute-start | bytes 245768 | tf_op jit(solution)/shard_map/ppermute | solution.py:638
  34.2 6.0 %collective-permute-start.3 = (s16[320,128]{1,0:T(8,128)(2,1)S(1)}, s16[320,128]{1,0:T(8,128)(2,1)S(1)}, u32[]{:S(2)}, u32[]{:S(2)}) collective-permute-start(s16[320,128]{1,0:T(8,128)(2,1)S(1)} %get-tuple-element.24), channel_id=1, source_target_pairs={{0,2},{1,3},{2,6},{3,7},{4,0},{5,1},{6,10},{7,11},{8,4},{9,5},{10,... | collective-permute-start | bytes 245768 | tf_op jit(solution)/shard_map/ppermute | solution.py:638
  36.2 4.0 %collective-permute-start = (s16[160,128]{1,0:T(8,128)(2,1)S(1)}, s16[160,128]{1,0:T(8,128)(2,1)S(1)}, u32[]{:S(2)}, u32[]{:S(2)}) collective-permute-start(s16[160,128]{1,0:T(8,128)(2,1)S(1)} %get-tuple-element.21), channel_id=1, source_target_pairs={{0,16},{1,0},{2,18},{3,2},{4,20},{5,4},{6,22},{7,6},{8,24},{9,8},{... | collective-permute-start | bytes 122888 | tf_op jit(solution)/shard_map/ppermute | solution.py:638
  36.2 4.0 %collective-permute-start.1 = (s16[160,128]{1,0:T(8,128)(2,1)S(1)}, s16[160,128]{1,0:T(8,128)(2,1)S(1)}, u32[]{:S(2)}, u32[]{:S(2)}) collective-permute-start(s16[160,128]{1,0:T(8,128)(2,1)S(1)} %get-tuple-element.22), channel_id=1, source_target_pairs={{0,1},{1,17},{2,3},{3,19},{4,5},{5,21},{6,7},{7,23},{8,9},{9,25},{... | collective-permute-start | bytes 122888 | tf_op jit(solution)/shard_map/ppermute | solution.py:638

commit v5 on v4

--- a/solution.py
+++ b/solution.py
@@ -253,6 +253,47 @@
     return shifted
 
 
+def ends(plan):
+    lane = lane_index(plan.xs)
+    row = lax.broadcasted_iota(jnp.int32, (plan.xs, LANES), 0)
+    return (
+        (row == 0, row == plan.xs - 1),
+        (lane < plan.side, lane >= LANES - plan.side),
+    )
+
+
+def sides_inner(plan, own):
+    (x_low, x_high), (y_low, y_high) = ends(plan)
+    side = plan.side
+    return [
+        ([roll_rows(t, 1) for t in own], x_low, [roll_rows(t, -1) for t in own], x_high),
+        ([roll_lanes(t, side) for t in own], y_low, [roll_lanes(t, -side) for t in own], y_high),
+    ]
+
+
+def states_outer(plan, table, kind, slot, own, x_halo, y_halo):
+    (x_low, _), (y_low, _) = ends(plan)
+    found = [table[(kind * COLUMNS + face) * plan.blocks + slot] for face in range(4)]
+    inside = [f >= 0 for f in found]
+    found = [jnp.maximum(f, 0) for f in found]
+    along_x, along_y = [], []
+    for v, tile in enumerate(own):
+        low = jnp.where(inside[0], x_halo(kind, found[0], v, 0), tile)
+        high = jnp.where(inside[1], x_halo(kind, found[1], v, 1), tile)
+        along_x.append(jnp.where(x_low, low, high))
+        low = jnp.where(inside[2], y_halo(kind, found[2], v, 0), tile)
+        high = jnp.where(inside[3], y_halo(kind, found[3], v, 1), tile)
+        along_y.append(jnp.where(y_low, low, high))
+    return along_x, along_y
+
+
+def at_ends(plan, low_value, high_value):
+    return [
+        jnp.where(low, low_value, jnp.where(high, high_value, 0.0)).astype(jnp.float32)
+        for low, high in ends(plan)
+    ]
+
+
 def primitives(conserved):
     density, energy = conserved[0], conserved[4]
     momentum = conserved[1:4]
@@ -324,8 +365,57 @@
     return total, [as_bf16(t) for t in cross(vorticity, velocity)]
 
 
+def les_inner(plan, table, slot, core, unit):
+    own = [core(0, slot, v) for v in range(plan.vars)]
+    part = les_z(plan, table, slot, core, unit)
+    total, velocity = part[: plan.vars], part[plan.vars + 2 :]
+    along_z = part[plan.vars : plan.vars + 2]
+    near, out = 0.5 * DT_LES * VISCOSITY, 0.25 * DT_LES
+    gradient = []
+    for axis, (low, low_end, high, high_end) in enumerate(sides_inner(plan, own)):
+        flux_low, speed_low = flux_along(low, axis)
+        flux_high, speed_high = flux_along(high, axis)
+        for v in range(plan.vars):
+            from_low = jnp.where(low_end, 0.0, near * low[v] + out * flux_low[v])
+            from_high = jnp.where(high_end, 0.0, near * high[v] - out * flux_high[v])
+            total[v] = total[v] + (from_low + from_high)
+        gradient.append(
+            [
+                jnp.where(high_end, 0.0, h) - jnp.where(low_end, 0.0, w)
+                for h, w in zip(speed_high, speed_low)
+            ]
+        )
+    along_x, along_y = gradient
+    vorticity = [along_y[2] - along_z[1], along_z[0] - along_x[2], along_x[1] - along_y[0]]
+    return total + vorticity + velocity
+
+
+def les_outer(plan, part, states):
+    count = plan.vars
+    total, vorticity, velocity = part[:count], part[count : count + 3], part[count + 3 :]
+    near = at_ends(plan, 0.5 * DT_LES * VISCOSITY, 0.5 * DT_LES * VISCOSITY)
+    out = at_ends(plan, 0.25 * DT_LES, -0.25 * DT_LES)
+    sign = at_ends(plan, -1.0, 1.0)
+    gradient = []
+    for axis, state in enumerate(states):
+        flux, speed = flux_along(state, axis)
+        total = [t + (near[axis] * g + out[axis] * f) for t, g, f in zip(total, state, flux)]
+        gradient.append([sign[axis] * u for u in speed])
+    along_x, along_y = gradient
+    vorticity = [
+        vorticity[0] + along_y[2],
+        vorticity[1] - along_x[2],
+        vorticity[2] + (along_x[1] - along_y[0]),
+    ]
+    return total, [as_bf16(t) for t in cross(vorticity, velocity)]
+
+
 def ac_axes(plan, total, axes, pairs, mean, source):
     slope = [[h - w for h, w in zip(high, low)] for low, high in pairs]
+    return ac_slopes(plan, total, axes, slope, mean, source)
+
+
+def ac_slopes(plan, total, axes, slope, mean, source):
     change = [None] * plan.vars
     divergence = None
     for axis, s in zip(axes, slope):
@@ -347,7 +437,28 @@
     return ac_axes(plan, [0.5 * g for g in own], (2,), [pair], mean(slot), None)
 
 
-def advance(plan, table, core, x_halo, y_halo, mean, lamb, les_part, ac_part, store):
+def ac_inner(plan, table, slot, core, mean):
+    own = [core(1, slot, v) for v in range(plan.vars)]
+    slope = []
+    for low, low_end, high, high_end in sides_inner(plan, own):
+        slope.append(
+            [
+                jnp.where(high_end, 0.0, h) - jnp.where(low_end, 0.0, w)
+                for h, w in zip(high, low)
+            ]
+        )
+    low, high = sides_z(plan, table, 1, slot, own, core)
+    slope.append([h - w for h, w in zip(high, low)])
+    return ac_slopes(plan, [0.5 * g for g in own], (0, 1, 2), slope, mean(slot), None)
+
+
+def ac_outer(plan, part, states, mean, source):
+    sign = at_ends(plan, -1.0, 1.0)
+    slope = [[sign[axis] * g for g in state] for axis, state in enumerate(states)]
+    return ac_slopes(plan, part, (0, 1), slope, mean, source)
+
+
+def advance(plan, table, core, lamb, les, ac, store):
     xs = plan.xs
 
     def les_quad(quad, carry):
@@ -355,8 +466,7 @@
         for r in range(4):
             slot = quad * 4 + r
             own = [core(0, slot, v) for v in range(plan.vars)]
-            shifted = sides_xy(plan, table, 0, slot, own, x_halo, y_halo)
-            total, vector = les_xy(plan, les_part(slot), shifted)
+            total, vector = les(slot, own)
             for j in range(3):
                 lamb[slot, j * xs : (j + 1) * xs, :] = vector[j]
             results.append(total)
@@ -368,11 +478,9 @@
         for r in range(4):
             slot = quad * 4 + r
             own = [core(1, slot, v) for v in range(plan.vars)]
-            shifted = sides_xy(plan, table, 1, slot, own, x_halo, y_halo)
             partner = table[(COLUMNS + FACES) * plan.blocks + slot]
             source = [lamb[partner, j * xs : (j + 1) * xs, :] for j in range(3)]
-            pairs = [shifted[0:2], shifted[2:4]]
-            results.append(ac_axes(plan, ac_part(slot), (0, 1), pairs, mean(slot), source))
+            results.append(ac(slot, own, source))
         store(1, quad, results)
         return carry
 
@@ -468,34 +576,48 @@
         y_up_raw[where, :] = in_quarters(rest, 3)
         y_down_raw[where, :] = in_quarters(rest, 0)
 
-    def les_part(slot):
-        return les_z(plan, table, slot, core, SCALE_IN)
-
-    def ac_part(slot):
-        return ac_z(plan, table, slot, core, mean)
-
-    advance(plan, table, core, x_halo, y_halo, mean, lamb, les_part, ac_part, store)
+    def les(slot, own):
+        shifted = sides_xy(plan, table, 0, slot, own, x_halo, y_halo)
+        return les_xy(plan, les_z(plan, table, slot, core, SCALE_IN), shifted)
+
+    def ac(slot, own, source):
+        shifted = sides_xy(plan, table, 1, slot, own, x_halo, y_halo)
+        pairs = [shifted[0:2], shifted[2:4]]
+        part = ac_z(plan, table, slot, core, mean)
+        return ac_axes(plan, part, (0, 1), pairs, mean(slot), source)
+
+    advance(plan, table, core, lamb, les, ac, store)
     for raw, out in (
         (x_up_raw, x_up), (x_down_raw, x_down), (y_up_raw, y_up), (y_down_raw, y_down),
     ):
         out[...] = to_wire(raw[...])
 
 
-def middle_kernel(plan, table, before, mean_in, les_out, ac_out):
+def middle_les_kernel(plan, table, before, out):
     def core(kind, slot, v):
         return before[kind * plan.blocks + slot, tile_rows(plan, v), :]
 
+    def body(slot, carry):
+        for i, tile in enumerate(les_inner(plan, table, slot, core, SCALE_MID)):
+            out[slot, tile_rows(plan, i), :] = tile
+        return carry
+
+    lax.fori_loop(0, plan.blocks, body, 0, unroll=4)
+
+
+def middle_ac_kernel(plan, table, before, mean_in, out):
+    def core(kind, slot, v):
+        return before[kind * plan.blocks + slot, tile_rows(plan, v), :]
+
     def mean(slot):
         return [mean_in[slot, tile_rows(plan, v), :] for v in range(plan.vars)]
 
     def body(slot, carry):
-        for i, tile in enumerate(les_z(plan, table, slot, core, SCALE_MID)):
-            les_out[slot, tile_rows(plan, i), :] = tile
-        for v, tile in enumerate(ac_z(plan, table, slot, core, mean)):
-            ac_out[slot, tile_rows(plan, v), :] = tile
+        for v, tile in enumerate(ac_inner(plan, table, slot, core, mean)):
+            out[slot, tile_rows(plan, v), :] = tile
         return carry
 
-    lax.fori_loop(0, plan.blocks, body, 0, unroll=2)
+    lax.fori_loop(0, plan.blocks, body, 0, unroll=4)
 
 
 def last_kernel(
@@ -523,7 +645,7 @@
     def y_halo(kind, slot, v, end):
         raw = y_high_raw if end else y_low_raw
         m = kind * blocks + slot
-        target = 0 if end else 3 * side
+        target = 3 * side if end else 0
         if v < 4:
             tile = raw[pl.ds(pl.multiple_of(m * xs, xs), xs), :]
             tile = roll_lanes(tile, target - side * v)
@@ -543,13 +665,16 @@
                 tile = tile if offset == 0.0 else tile - offset
                 coded[kind * blocks + quad * 4 + r, tile_rows(plan, v), :] = tile
 
-    def les_part(slot):
-        return [les_in[slot, tile_rows(plan, i), :] for i in range(count + 5)]
-
-    def ac_part(slot):
-        return [ac_in[slot, tile_rows(plan, v), :] for v in range(count)]
-
-    advance(plan, table, core, x_halo, y_halo, mean, lamb, les_part, ac_part, store)
+    def les(slot, own):
+        part = [les_in[slot, tile_rows(plan, i), :] for i in range(count + 6)]
+        return les_outer(plan, part, states_outer(plan, table, 0, slot, own, x_halo, y_halo))
+
+    def ac(slot, own, source):
+        part = [ac_in[slot, tile_rows(plan, v), :] for v in range(count)]
+        states = states_outer(plan, table, 1, slot, own, x_halo, y_halo)
+        return ac_outer(plan, part, states, mean(slot), source)
+
+    advance(plan, table, core, lamb, les, ac, store)
 
     def write(m, carry):
         message[m] = to_wire(coded[m])
@@ -637,15 +762,20 @@
     moves = [plan.permutation(*step) for step in ((1, 0), (-1, 0), (0, 1), (0, -1))]
     halos = [lax.ppermute(halo, axes, move) for halo, move in zip(halos, moves)]
 
-    parts = pl.pallas_call(
-        functools.partial(middle_kernel, plan),
-        out_shape=(
-            array(f32, blocks, (count + 5) * xs, LANES),
-            array(f32, blocks, plan.core_rows, LANES),
-        ),
+    les_part = pl.pallas_call(
+        functools.partial(middle_les_kernel, plan),
+        out_shape=array(f32, blocks, (count + 6) * xs, LANES),
+        in_specs=smem(1) + vmem(1),
+        out_specs=vmem(1)[0],
+        name="middle_les",
+        compiler_params=pltpu.CompilerParams(vmem_limit_bytes=16 * 1024 * 1024),
+    )(table, after)
+    ac_part = pl.pallas_call(
+        functools.partial(middle_ac_kernel, plan),
+        out_shape=array(f32, blocks, plan.core_rows, LANES),
         in_specs=smem(1) + vmem(2),
-        out_specs=tuple(vmem(2)),
-        name="middle",
+        out_specs=vmem(1)[0],
+        name="middle_ac",
         compiler_params=pltpu.CompilerParams(vmem_limit_bytes=16 * 1024 * 1024),
     )(table, after, mean)
     message = pl.pallas_call(
@@ -658,7 +788,7 @@
         + [pltpu.VMEM((devices, plan.core_rows, LANES), f32)],
         name="last_step",
         compiler_params=pltpu.CompilerParams(vmem_limit_bytes=16 * 1024 * 1024),
-    )(table, after, mean, *parts, *halos)
+    )(table, after, mean, les_part, ac_part, *halos)
     message = lax.all_to_all(message, axes, split_axis=0, concat_axis=0, tiled=True)
 
     result = pl.pallas_call(

time: 58.2 us -> 57.5 us (0.988)
    pallas_call x1, Pallas kernels: 1.79 us -> 1.11 us  [on_device(): pl.pallas_call(functools.partial(last_kernel, plan), out_shape=array(WIRE...]
    pallas_call x1 -> x2, Pallas kernels: 0.92 us -> 1.41 us  [the longest x1 0.78 us: on_device(): pl.pallas_call(functools.partial(middle_les_kernel, plan), out_shape=arra...]
where the time goes in v5:
time: 57.5 us; the launch traced here: 57.3 us
  blocking collectives  44.6 us (78%)
  Pallas kernels  8.02 us (14%)
  starting transfers between devices  4.1 us (7%)
    all_to_all x2, blocking collectives, on_device(): lax.all_to_all(message, axes, split_axis=0, concat_axis=0, tiled=True)  44.6 us
    ppermute x4, starting transfers between devices, on_device(): halos = [lax.ppermute(halo, axes, move) for halo, move in zip(halos, moves)]  4.1 us
    pallas_call x1, Pallas kernels, on_device(): pl.pallas_call(functools.partial(first_kernel, plan), out_shape=(array(f3...  2.71 us
    pallas_call x1, Pallas kernels, on_device(): pl.pallas_call(functools.partial(pack_kernel, plan), out_shape=(array(WIR...  1.86 us
  transfers between devices with their start and end apart: 4, of which 1 were waited for; matrix products, arithmetic and copies ran while one was open for 0% of the time, Pallas kernels for 2%

profile of v5, /device:TPU:0, one launch (start us, length us, event | category | flops | bytes accessed | tf_op | source)
XLA Modules:
  0.0 57.3 jit_solution(14868540378639216995)
XLA Ops:
  0.0 1.9 %pack.1 = (s16[32,96,128]{2,1,0:T(8,128)(2,1)S(1)}, s32[224]{0:T(256)S(4)}) custom-call(f32[5,32,1024]{2,1,0:T(8,128)} %bitcast.5, f32[5,32,1024]{2,1,0:T(8,128)} %bitcast.6, s32[16]{0:T(128)} %refs_0_.1, s32[16]{0:T(128)} %refs_1_.1, s32[6,16]{1,0:T(8,128)} %bitcast.7, s32[6,16]{1,0:T(8,128)} %bitcast.8, s32[16]{0:T(128)} %refs_4_.1), custom_call_target="tpu_custom_call" | custom-call | tf_op jit(solution)/shard_map/pack/pallas_call | solution.py:721
  1.9 29.6 %all_to_all.10.message = s16[32,96,128]{2,1,0:T(8,128)(2,1)S(1)} all-to-all(s16[32,96,128]{2,1,0:T(8,128)(2,1)S(1)} %get-tuple-element.14), channel_id=1, replica_groups=mesh['section'=2,'block'=16] {'section','block'}, dimensions={0} | all-to-all | bytes 1572864 | tf_op jit(solution)/shard_map/all_to_all | solution.py:737
  31.4 2.7 %first_step.1 = (f32[32,40,128]{2,1,0:T(8,128)S(1)}, f32[16,40,128]{2,1,0:T(8,128)S(1)}, s16[160,128]{1,0:T(8,128)(2,1)S(1)}, s16[160,128]{1,0:T(8,128)(2,1)S(1)...) custom-call(s32[224]{0:T(256)S(4)} %get-tuple-element.13.table, s16[32,96,128]{2,1,0:T(8,128)(2,1)S(1)} %all_to_all.10.message), custom_call_target="tpu_custom_call" | custom-call | tf_op jit(solution)/shard_map/first_step/pallas_call | solution.py:744
  34.1 0.1 collective-permute-start.2
  34.2 2.0 %collective-permute-start.3 = (s16[320,128]{1,0:T(8,128)(2,1)S(1)}, s16[320,128]{1,0:T(8,128)(2,1)S(1)}, u32[]{:S(2)}, u32[]{:S(2)}) collective-permute-start(s16[320,128]{1,0:T(8,128)(2,1)S(1)} %get-tuple-element.20), channel_id=1, source_target_pairs={{0,2},{1,3},{2,6},{3,7},{4,0},{5,1},{6,10},{7,11},{8,4},{9,5},{10,... | collective-permute-start | bytes 245768 | tf_op jit(solution)/shard_map/ppermute | solution.py:763
  36.2 0.0 collective-permute-start
  36.2 2.0 %collective-permute-start.1 = (s16[160,128]{1,0:T(8,128)(2,1)S(1)}, s16[160,128]{1,0:T(8,128)(2,1)S(1)}, u32[]{:S(2)}, u32[]{:S(2)}) collective-permute-start(s16[160,128]{1,0:T(8,128)(2,1)S(1)} %get-tuple-element.18), channel_id=1, source_target_pairs={{0,1},{1,17},{2,3},{3,19},{4,5},{5,21},{6,7},{7,23},{8,9},{9,25},{... | collective-permute-start | bytes 122888 | tf_op jit(solution)/shard_map/ppermute | solution.py:763
  38.3 0.8 %middle_les.1.les_in = f32[16,88,128]{2,1,0:T(8,128)S(1)} custom-call(s32[224]{0:T(256)S(4)} %get-tuple-element.13.table, f32[32,40,128]{2,1,0:T(8,128)S(1)} %get-tuple-element.15.before), custom_call_target="tpu_custom_call" | custom-call | tf_op jit(solution)/shard_map/middle_les/pallas_call | solution.py:765
  39.0 0.6 %middle_ac.1.ac_in = f32[16,40,128]{2,1,0:T(8,128)S(1)} custom-call(s32[224]{0:T(256)S(4)} %get-tuple-element.13.table, f32[32,40,128]{2,1,0:T(8,128)S(1)} %get-tuple-element.15.before, f32[16,40,128]{2,1,0:T(8,128)S(1)} %get-tuple-element.16.mean_in), custom_call_target="tpu_custom_call" | custom-call | tf_op jit(solution)/shard_map/middle_ac/pallas_call | solution.py:773
  39.7 0.6 collective-permute-done.x_low
  40.2 0.0 collective-permute-done.1.x_high
  40.2 0.0 collective-permute-done.2.y_low
  40.2 0.0 collective-permute-done.3.y_high
  40.2 1.1 %last_step.1 = s16[32,40,128]{2,1,0:T(8,128)(2,1)S(1)} custom-call(s32[224]{0:T(256)S(4)} %get-tuple-element.13.table, f32[32,40,128]{2,1,0:T(8,128)S(1)} %get-tuple-element.15.before, f32[16,40,128]{2,1,0:T(8,128)S(1)} %get-tuple-element.16.mean_in, f32[16,88,128]{2,1,0:T(8,128)S(1)} %middle_les.1.les_in, f32[16,40,128]{2,1,0:T(8,128)S(1)} %middle_ac.1.ac_in, ...), custom_call_target="tpu_custom_call" | custom-call | tf_op jit(solution)/shard_map/last_step/pallas_call | solution.py:781
  41.4 15.1 %all_to_all.11.message = s16[32,40,128]{2,1,0:T(8,128)(2,1)S(1)} all-to-all(s16[32,40,128]{2,1,0:T(8,128)(2,1)S(1)} %last_step.1), channel_id=1, replica_groups=mesh['section'=2,'block'=16] {'section','block'}, dimensions={0} | all-to-all | bytes 655360 | tf_op jit(solution)/shard_map/all_to_all | solution.py:792
  56.4 0.9 %unpack.1 = f32[5,32,1024]{2,1,0:T(8,128)} custom-call(s16[32,40,128]{2,1,0:T(8,128)(2,1)S(1)} %all_to_all.11.message), custom_call_target="tpu_custom_call" | custom-call | tf_op jit(solution)/shard_map/unpack/pallas_call | solution.py:794
Async XLA Ops:
  34.1 6.1 %collective-permute-start.2 = (s16[320,128]{1,0:T(8,128)(2,1)S(1)}, s16[320,128]{1,0:T(8,128)(2,1)S(1)}, u32[]{:S(2)}, u32[]{:S(2)}) collective-permute-start(s16[320,128]{1,0:T(8,128)(2,1)S(1)} %get-tuple-element.19), channel_id=1, source_target_pairs={{0,4},{1,5},{2,0},{3,1},{4,8},{5,9},{6,2},{7,3},{8,12},{9,13},{10,... | collective-permute-start | bytes 245768 | tf_op jit(solution)/shard_map/ppermute | solution.py:763
  34.2 6.0 %collective-permute-start.3 = (s16[320,128]{1,0:T(8,128)(2,1)S(1)}, s16[320,128]{1,0:T(8,128)(2,1)S(1)}, u32[]{:S(2)}, u32[]{:S(2)}) collective-permute-start(s16[320,128]{1,0:T(8,128)(2,1)S(1)} %get-tuple-element.20), channel_id=1, source_target_pairs={{0,2},{1,3},{2,6},{3,7},{4,0},{5,1},{6,10},{7,11},{8,4},{9,5},{10,... | collective-permute-start | bytes 245768 | tf_op jit(solution)/shard_map/ppermute | solution.py:763
  36.2 4.0 %collective-permute-start = (s16[160,128]{1,0:T(8,128)(2,1)S(1)}, s16[160,128]{1,0:T(8,128)(2,1)S(1)}, u32[]{:S(2)}, u32[]{:S(2)}) collective-permute-start(s16[160,128]{1,0:T(8,128)(2,1)S(1)} %get-tuple-element.17), channel_id=1, source_target_pairs={{0,16},{1,0},{2,18},{3,2},{4,20},{5,4},{6,22},{7,6},{8,24},{9,8},{... | collective-permute-start | bytes 122888 | tf_op jit(solution)/shard_map/ppermute | solution.py:763
  36.2 4.0 %collective-permute-start.1 = (s16[160,128]{1,0:T(8,128)(2,1)S(1)}, s16[160,128]{1,0:T(8,128)(2,1)S(1)}, u32[]{:S(2)}, u32[]{:S(2)}) collective-permute-start(s16[160,128]{1,0:T(8,128)(2,1)S(1)} %get-tuple-element.18), channel_id=1, source_target_pairs={{0,1},{1,17},{2,3},{3,19},{4,5},{5,21},{6,7},{7,23},{8,9},{9,25},{... | collective-permute-start | bytes 122888 | tf_op jit(solution)/shard_map/ppermute | solution.py:763
